TPU v7x, 32 devices: a whole 2x2x4 slice. The times are simulated.
32 devices in a mesh: dp: 8 (over z, y), shard: 4 (over x, core).
Axes of the slice: x: 2, y: 2, z: 4, core: 2. Of those that a mesh axis runs over, the one named last changes fastest.
Arguments:
- tokens_in: bfloat16 [4096, 1088], P(('dp', 'shard')), may hold values from -6 to 6
- cotangent: bfloat16 [4096, 1088], P(('dp', 'shard')), may hold values from -6 to 6
- segment_ids: int32 [4096], P('dp'), may hold values from -1 to 3, as said below
- w_qkv: float32 [1088, 3264], P('shard', 'dp'), may hold values from -0.1875 to 0.1875
- w_attn_out: float32 [1088, 1088], P('shard', 'dp'), may hold values from -0.75 to 0.75
- w_fc: float32 [1088, 4352], P('shard', 'dp'), may hold values from -0.1875 to 0.1875
- w_proj: float32 [4352, 1088], P('shard', 'dp'), may hold values from -0.09375 to 0.09375
- small_w: float32 [12, 1088], P(None, 'shard'), may hold values from -0.8 to 1.8
- moment_qkv: float32 [1088, 3264], P('shard', 'dp'), may hold values from -8 to 8
- moment_attn_out: float32 [1088, 1088], P('shard', 'dp'), may hold values from -8 to 8
- moment_fc: float32 [1088, 4352], P('shard', 'dp'), may hold values from -8 to 8
- moment_proj: float32 [4352, 1088], P('shard', 'dp'), may hold values from -8 to 8
- moment_small: float32 [12, 1088], P(None, 'shard'), may hold values from -8 to 8
- second_qkv: float32 [1088, 3264], P('shard', 'dp'), may hold values from 128 to 512
- second_attn_out: float32 [1088, 1088], P('shard', 'dp'), may hold values from 128 to 512
- second_fc: float32 [1088, 4352], P('shard', 'dp'), may hold values from 128 to 512
- second_proj: float32 [4352, 1088], P('shard', 'dp'), may hold values from 128 to 512
- second_small: float32 [12, 1088], P(None, 'shard'), may hold values from 128 to 512
Outputs:
- out_act: bfloat16 [4096, 1088], P(('dp', 'shard'))
- grad_input: bfloat16 [4096, 1088], P(('dp', 'shard'))
- grad_qkv: float32 [1088, 3264], P('shard', 'dp')
- grad_attn_out: float32 [1088, 1088], P('shard', 'dp')
- grad_fc: float32 [1088, 4352], P('shard', 'dp')
- grad_proj: float32 [4352, 1088], P('shard', 'dp')
- grad_small: float32 [12, 1088], P(None, 'shard')
- new_qkv: float32 [1088, 3264], P('shard', 'dp')
- new_attn_out: float32 [1088, 1088], P('shard', 'dp')
- new_fc: float32 [1088, 4352], P('shard', 'dp')
- new_proj: float32 [4352, 1088], P('shard', 'dp')
- new_small: float32 [12, 1088], P(None, 'shard')
- new_moment_qkv: float32 [1088, 3264], P('shard', 'dp')
- new_moment_attn_out: float32 [1088, 1088], P('shard', 'dp')
- new_moment_fc: float32 [1088, 4352], P('shard', 'dp')
- new_moment_proj: float32 [4352, 1088], P('shard', 'dp')
- new_moment_small: float32 [12, 1088], P(None, 'shard')
- new_second_qkv: float32 [1088, 3264], P('shard', 'dp')
- new_second_attn_out: float32 [1088, 1088], P('shard', 'dp')
- new_second_fc: float32 [1088, 4352], P('shard', 'dp')
- new_second_proj: float32 [4352, 1088], P('shard', 'dp')
- new_second_small: float32 [12, 1088], P(None, 'shard')
Inputs may be any that keep to these rules, and one draw needn't show every extreme that they name: `segment_ids`: within each group of 512 consecutive slots the ids number that group's sequences 0, 1, 2, ... in order and the group's first slot has id 0; each sequence begins at a multiple of 128, spans at most 4 blocks and ends inside its last block; -1 marks padding slots after a sequence's end. In the first group every block starts a sequence.
All inputs are finite; a program needn't handle non-finite values.
Results may differ from a plain program's by a relative error of at most 0.022.
Values may be sent and summed in bfloat16 or wider, within the bound.
A program may use at most 192 MiB of HBM per device.

v0:
```python
import math

import jax
import jax.numpy as jnp
from jax import lax
from jax.experimental import pallas as pl
from jax.experimental.pallas import tpu as pltpu
from jax.sharding import PartitionSpec as P

D = 1088
H = 17
HD = 64
FF = 4352
STEP = 3


NORM_EPS = 1e-05
LEARN_RATE = 0.01
BETA_ONE = 0.9
BETA_TWO = 0.95
ADAM_EPS = 1e-08
WEIGHT_DECAY = 0.1


def outer_sum(left_rows, right_rows):
    return lax.dot_general(
        left_rows, right_rows, (((0,), (0,)), ((), ())), preferred_element_type=jnp.float32
    )


def back_product(left_rows, right_rows):
    return lax.dot_general(
        left_rows, right_rows, (((1,), (1,)), ((), ())), preferred_element_type=jnp.float32
    )


def matmul(left_rows, right_rows):
    return jnp.dot(left_rows, right_rows, preferred_element_type=jnp.float32)


def norm_forward(row_data, gain_row, shift_row):
    row_mean = jnp.mean(row_data, axis=-1, keepdims=True)
    centered = row_data - row_mean
    variance = jnp.mean(centered * centered, axis=-1, keepdims=True)
    inverse_dev = lax.rsqrt(variance + NORM_EPS)
    normed = centered * inverse_dev
    return (normed, inverse_dev, normed * gain_row + shift_row)


def norm_backward(grad_rows, normed, inverse_dev, gain_row):
    scaled = grad_rows * gain_row
    return inverse_dev * (
        scaled
        - jnp.mean(scaled, axis=-1, keepdims=True)
        - normed * jnp.mean(scaled * normed, axis=-1, keepdims=True)
    )


def gelu_slope(pre_act):
    normal_cdf = 0.5 * (1.0 + lax.erf(pre_act * 0.7071067811865476))
    normal_pdf = jnp.exp(-0.5 * pre_act * pre_act) * 0.3989422804014327
    return normal_cdf + pre_act * normal_pdf


def head_split(rows_in):
    return rows_in.reshape(rows_in.shape[0], H, HD)


def prob_table(queries, key_rows, allowed, log_total):
    score_scale = 1.0 / math.sqrt(HD)
    scores = (
        jnp.einsum(
            "rhe,khe->hrk",
            head_split(queries),
            head_split(key_rows),
            preferred_element_type=jnp.float32,
        )
        * score_scale
    )
    if log_total is None:
        exp_scores = jnp.where(allowed[None], jnp.exp(scores), 0.0)
        log_total = jnp.log(jnp.sum(exp_scores, axis=-1))
    prob_full = jnp.where(allowed[None], jnp.exp(scores - log_total[..., None]), 0.0)
    return (prob_full, log_total)


def attend_forward(queries, key_rows, value_rows, allowed):
    prob_full, log_total = prob_table(queries, key_rows, allowed, None)
    prob_half = prob_full.astype(jnp.bfloat16)
    attended = jnp.einsum(
        "hrk,khe->rhe", prob_half, head_split(value_rows), preferred_element_type=jnp.float32
    )
    return (attended.reshape(queries.shape[0], H * HD).astype(jnp.bfloat16), log_total)


def attend_backward(queries, key_rows, value_rows, allowed, log_total, attended, grad_attn):
    row_count = queries.shape[0]
    key_count = key_rows.shape[0]
    score_scale = 1.0 / math.sqrt(HD)
    prob_full, unused_total = prob_table(queries, key_rows, allowed, log_total)
    prob_half = prob_full.astype(jnp.bfloat16)
    grad_heads = head_split(grad_attn)
    row_delta = jnp.sum(
        grad_heads.astype(jnp.float32) * head_split(attended).astype(jnp.float32), axis=-1
    )
    d_probs = jnp.einsum(
        "rhe,khe->hrk", grad_heads, head_split(value_rows), preferred_element_type=jnp.float32
    )
    d_scores = prob_full * (d_probs - jnp.transpose(row_delta)[..., None])
    grad_scores = (d_scores * score_scale).astype(jnp.bfloat16)
    d_query = jnp.einsum(
        "hrk,khe->rhe", grad_scores, head_split(key_rows), preferred_element_type=jnp.float32
    ).reshape(row_count, H * HD)
    d_keys = jnp.einsum(
        "hrk,rhe->khe", grad_scores, head_split(queries), preferred_element_type=jnp.float32
    ).reshape(key_count, H * HD)
    d_values = jnp.einsum(
        "hrk,rhe->khe", prob_half, grad_heads, preferred_element_type=jnp.float32
    ).reshape(key_count, H * HD)
    return (d_query, d_keys, d_values)


def adam_update(weight, moment_one, moment_two, gradient, decay_rate):
    moment_new = BETA_ONE * moment_one + (1.0 - BETA_ONE) * gradient
    second_new = BETA_TWO * moment_two + (1.0 - BETA_TWO) * gradient * gradient
    moment_hat = moment_new / (1.0 - BETA_ONE**STEP)
    second_hat = second_new / (1.0 - BETA_TWO**STEP)
    weight_new = weight - LEARN_RATE * (
        moment_hat / (jnp.sqrt(second_hat) + ADAM_EPS) + decay_rate * weight
    )
    return (weight_new, moment_new, second_new)


LANES = 128


def pad_rows(rows_in, count):
    return jnp.pad(rows_in, ((0, count - rows_in.shape[0]), (0, 0)))


def eight(count):
    return -(-count // 8) * 8


def tiles_of(piece):
    blocks = piece.shape[1] // LANES
    return jnp.concatenate(
        [piece[:, i * LANES : (i + 1) * LANES] for i in range(blocks)], axis=0
    )


def rest_rows(count, width):
    return -(-count // (LANES // width)) if width else 0


def rest_of(rest):
    count, width = rest.shape[-2:]
    fold = LANES // width
    rows = rest_rows(count, width)
    lead = rest.shape[:-2]
    rest = jnp.pad(rest, [(0, 0)] * len(lead) + [(0, fold * rows - count), (0, 0)])
    return jnp.swapaxes(rest.reshape(lead + (fold, rows, width)), -3, -2).reshape(
        lead + (rows, LANES)
    )


def rest_back(packed, count, width):
    fold = LANES // width
    lead, rows = packed.shape[:-2], packed.shape[-2]
    rest = jnp.swapaxes(packed.reshape(lead + (rows, fold, width)), -3, -2)
    return rest.reshape(lead + (fold * rows, width))[..., :count, :]


def by_shard(rows_in, parts):
    width = rows_in.shape[1] // parts
    main = width // LANES * LANES
    cuts = [rows_in[:, i * width : i * width + main] for i in range(parts)]
    cuts += [rows_in[:, i * width + main : (i + 1) * width] for i in range(parts)]
    return jnp.concatenate(cuts, axis=1)


def by_index(rows_in, parts):
    width = rows_in.shape[1] // parts
    main = width // LANES * LANES
    rest = width - main
    cuts = []
    for i in range(parts):
        cuts.append(rows_in[:, i * main : (i + 1) * main])
        cuts.append(rows_in[:, parts * main + i * rest : parts * main + (i + 1) * rest])
    return jnp.concatenate(cuts, axis=1)


def join_kernel(plan, tiles_ref, *refs):
    rest_refs, out_refs = refs[: len(plan)], refs[len(plan) :]
    for (start, count, blocks), rest_ref, out_ref in zip(plan, rest_refs, out_refs):
        parts = tiles_ref.shape[1]
        for i in range(parts):
            for j in range(blocks):
                lane = (i * blocks + j) * LANES
                out_ref[0, :, lane : lane + LANES] = tiles_ref[
                    0, i, start + j * count : start + (j + 1) * count, :
                ]
        out_ref[0, :, parts * blocks * LANES :] = rest_ref[0]


def join_tiles(gathered, plan, rests):
    n_dp, parts, rows, lanes = gathered.shape
    shapes = [
        (n_dp, count, parts * blocks * LANES + rest.shape[-1])
        for (start, count, blocks), rest in zip(plan, rests)
    ]
    return pl.pallas_call(
        lambda *refs: join_kernel(plan, *refs),
        grid=(n_dp,),
        in_specs=[pl.BlockSpec((1, parts, rows, lanes), lambda d: (d, 0, 0, 0))]
        + [pl.BlockSpec((1,) + rest.shape[1:], lambda d: (d, 0, 0)) for rest in rests],
        out_specs=[pl.BlockSpec((1,) + shape[1:], lambda d: (d, 0, 0)) for shape in shapes],
        out_shape=[jax.ShapeDtypeStruct(shape, gathered.dtype) for shape in shapes],
        compiler_params=pltpu.CompilerParams(vmem_limit_bytes=40 * 1024 * 1024),
    )(gathered, *rests)


def cut_kernel(plan, rest_starts, *refs):
    pairs = len(plan)
    left_refs, right_refs = refs[:pairs], refs[pairs : 2 * pairs]
    rest_refs, out_ref = refs[2 * pairs : -1], refs[-1]
    parts = out_ref.shape[1]
    for (start, count, blocks), left_ref, right_ref in zip(plan, left_refs, right_refs):
        for i in range(parts):
            width = blocks * LANES
            product = jnp.dot(
                left_ref[0],
                right_ref[:, i * width : (i + 1) * width],
                preferred_element_type=jnp.float32,
            ).astype(out_ref.dtype)
            for j in range(blocks):
                out_ref[0, i, start + j * count : start + (j + 1) * count, :] = product[
                    :, j * LANES : (j + 1) * LANES
                ]
    for start, rest_ref in zip(rest_starts, rest_refs):
        for i in range(parts):
            out_ref[0, i, start : start + rest_ref.shape[2], :] = rest_ref[0, i]


def cut_tiles(left_list, right_list, plan, rest_list, rest_starts, rows):
    n_dp, parts = rest_list[0].shape[:2]
    lefts = [
        left.T.reshape(n_dp, count, left.shape[0])
        for left, (start, count, blocks) in zip(left_list, plan)
    ]
    return pl.pallas_call(
        lambda *refs: cut_kernel(plan, rest_starts, *refs),
        grid=(n_dp,),
        in_specs=[pl.BlockSpec((1,) + left.shape[1:], lambda d: (d, 0, 0)) for left in lefts]
        + [pl.BlockSpec(right.shape, lambda d: (0, 0)) for right in right_list]
        + [pl.BlockSpec((1,) + rest.shape[1:], lambda d: (d, 0, 0, 0)) for rest in rest_list],
        out_specs=pl.BlockSpec((1, parts, rows, LANES), lambda d: (d, 0, 0, 0)),
        out_shape=jax.ShapeDtypeStruct((n_dp, parts, rows, LANES), jnp.bfloat16),
        compiler_params=pltpu.CompilerParams(vmem_limit_bytes=40 * 1024 * 1024),
    )(*lefts, *right_list, *rest_list)


def on_device(
    tokens_in,
    cotangent,
    segment_ids,
    w_qkv,
    w_attn_out,
    w_fc,
    w_proj,
    small_w,
    moment_qkv,
    moment_attn_out,
    moment_fc,
    moment_proj,
    moment_small,
    second_qkv,
    second_attn_out,
    second_fc,
    second_proj,
    second_small,
):
    axes = ("dp", "shard")
    n_dp = lax.axis_size("dp")
    n_shard = lax.axis_size("shard")
    rows_own, cols_qkv = w_qkv.shape
    cols_out = w_attn_out.shape[1]
    cols_fc = w_fc.shape[1]
    cols_proj = w_proj.shape[1]
    rows_proj = w_proj.shape[0]
    main_own = rows_own // LANES * LANES
    main_proj = rows_proj // LANES * LANES
    rest_own, rest_proj = rows_own - main_own, rows_proj - main_proj
    col_list = (cols_qkv, cols_out, cols_fc)
    col_sum = sum(col_list)
    sizes = [count * (main_own // LANES) for count in col_list]
    sizes += [cols_proj * (main_proj // LANES)]
    sizes += [eight(rest_rows(col_sum, rest_own)), eight(rest_rows(cols_proj, rest_proj))]
    starts = [sum(sizes[:i]) for i in range(len(sizes) + 1)]
    pieces = [w.astype(jnp.bfloat16).T for w in (w_qkv, w_attn_out, w_fc)]
    piece_proj = w_proj.astype(jnp.bfloat16).T
    rest_one = jnp.concatenate([piece[:, main_own:] for piece in pieces], axis=0)
    small_count = small_w.shape[0] * rows_own
    small_tiles = eight(-(-small_count // LANES))
    small_flat = jnp.pad(
        small_w.astype(jnp.bfloat16).reshape(small_count), (0, small_tiles * LANES - small_count)
    )
    packed = jnp.concatenate(
        [tiles_of(piece[:, :main_own]) for piece in pieces]
        + [
            tiles_of(piece_proj[:, :main_proj]),
            pad_rows(rest_of(rest_one), sizes[4]),
            pad_rows(rest_of(piece_proj[:, main_proj:]), sizes[5]),
            small_flat.reshape(small_tiles, LANES),
        ],
        axis=0,
    )
    gathered = lax.all_gather(packed, axes, axis=0, tiled=False).reshape(
        n_dp, n_shard, packed.shape[0], LANES
    )

    def rows_at(start, count):
        return lax.slice_in_dim(gathered, start, start + count, axis=2)

    all_rest = jnp.swapaxes(
        rest_back(rows_at(starts[4], rest_rows(col_sum, rest_own)), col_sum, rest_own), 1, 2
    ).reshape(n_dp, col_sum, n_shard * rest_own)

    proj_rest = jnp.swapaxes(
        rest_back(rows_at(starts[5], rest_rows(cols_proj, rest_proj)), cols_proj, rest_proj), 1, 2
    ).reshape(n_dp, cols_proj, n_shard * rest_proj)
    own_blocks = main_own // LANES
    plan = [
        (starts[0], cols_qkv, own_blocks),
        (starts[1], cols_out, own_blocks),
        (starts[2], cols_fc, own_blocks),
        (starts[3], cols_proj, main_proj // LANES),
    ]
    rests = [
        all_rest[:, :cols_qkv],
        all_rest[:, cols_qkv : cols_qkv + cols_out],
        all_rest[:, cols_qkv + cols_out :],
        proj_rest,
    ]
    full_qkv, full_out, full_fc, full_proj = (
        full.reshape(full.shape[0] * full.shape[1], full.shape[2])
        for full in join_tiles(gathered, plan, rests)
    )
    full_small = jnp.transpose(
        gathered[0, :, starts[6] :]
        .reshape(n_shard, small_tiles * LANES)[:, :small_count]
        .reshape(n_shard, small_w.shape[0], rows_own),
        (1, 0, 2),
    ).reshape(small_w.shape[0], n_shard * rows_own)
    small_vals = full_small.astype(jnp.float32)
    gain_one = small_vals[0]
    shift_one = small_vals[1]
    q_bias = small_vals[2]
    v_bias = small_vals[3]
    out_bias = small_vals[4]
    gain_two = small_vals[5]
    shift_two = small_vals[6]
    fc_bias = small_vals[7:11].reshape(FF)
    proj_bias = small_vals[11]
    tok_rows = tokens_in.shape[0]
    group_size = segment_ids.shape[0]
    shard_index = lax.axis_index("shard")
    own_seg = lax.dynamic_slice_in_dim(segment_ids, shard_index * tok_rows, tok_rows)
    query_pos = shard_index * tok_rows + jnp.arange(tok_rows, dtype=jnp.int32)
    x_rows = tokens_in.astype(jnp.float32)
    normed_one, inv_one, ln_one = norm_forward(x_rows, gain_one, shift_one)
    ln_one_half = ln_one.astype(jnp.bfloat16)
    ln_one_cut = by_shard(ln_one_half, n_shard)
    qkv_rows = back_product(ln_one_cut, full_qkv) + jnp.concatenate(
        [q_bias, jnp.zeros_like(q_bias), v_bias]
    )
    queries = qkv_rows[:, :D].astype(jnp.bfloat16)
    kv_half = qkv_rows[:, D:].astype(jnp.bfloat16)
    kv_all = lax.all_gather(kv_half, "shard", axis=0, tiled=True)
    key_all = kv_all[:, :D]
    value_all = kv_all[:, D:]
    key_pos = jnp.arange(group_size, dtype=jnp.int32)
    allowed = (
        (own_seg[:, None] == segment_ids[None, :])
        & (key_pos[None, :] <= query_pos[:, None])
        & ((own_seg >= 0)[:, None] | (key_pos[None, :] == query_pos[:, None]))
    )
    attended, log_total = attend_forward(queries, key_all, value_all, allowed)
    attended_cut = by_shard(attended, n_shard)
    resid = x_rows + back_product(attended_cut, full_out) + out_bias
    normed_two, inv_two, ln_two = norm_forward(resid, gain_two, shift_two)
    ln_two_half = ln_two.astype(jnp.bfloat16)
    ln_two_cut = by_shard(ln_two_half, n_shard)
    pre_act = back_product(ln_two_cut, full_fc) + fc_bias
    act_half = jax.nn.gelu(pre_act, approximate=False).astype(jnp.bfloat16)
    act_cut = by_shard(act_half, n_shard)
    out_act = (resid + back_product(act_cut, full_proj) + proj_bias).astype(jnp.bfloat16)
    valid = (own_seg >= 0).astype(jnp.float32)
    grad_z = cotangent.astype(jnp.float32) * valid[:, None]
    gz_half = grad_z.astype(jnp.bfloat16)
    d_pre = by_index(matmul(gz_half, full_proj), n_shard) * gelu_slope(pre_act)
    gu_half = d_pre.astype(jnp.bfloat16)
    d_ln_two = by_index(matmul(gu_half, full_fc), n_shard)
    d_resid = grad_z + norm_backward(d_ln_two, normed_two, inv_two, gain_two)
    gh_half = d_resid.astype(jnp.bfloat16)
    grad_attn = by_index(matmul(gh_half, full_out).astype(jnp.bfloat16), n_shard)
    d_query, d_keys_all, d_values_all = attend_backward(
        queries, key_all, value_all, allowed, log_total, attended, grad_attn
    )
    d_kv = lax.psum_scatter(
        jnp.concatenate(
            [d_keys_all.astype(jnp.bfloat16), d_values_all.astype(jnp.bfloat16)], axis=1
        ),
        "shard",
        scatter_dimension=0,
        tiled=True,
    )
    d_values = d_kv[:, D:].astype(jnp.float32)
    gqkv_half = jnp.concatenate([d_query.astype(jnp.bfloat16), d_kv], axis=1)
    d_ln_one = by_index(matmul(gqkv_half, full_qkv), n_shard)
    grad_input = (d_resid + norm_backward(d_ln_one, normed_one, inv_one, gain_one)).astype(
        jnp.bfloat16
    )
    small_rows = jnp.stack(
        [
            jnp.sum(d_ln_one * normed_one, axis=0),
            jnp.sum(d_ln_one, axis=0),
            jnp.sum(d_query, axis=0),
            jnp.sum(d_values, axis=0),
            jnp.sum(d_resid, axis=0),
            jnp.sum(d_ln_two * normed_two, axis=0),
            jnp.sum(d_ln_two, axis=0),
        ]
    )
    small_grad = jnp.concatenate(
        [small_rows, jnp.sum(d_pre, axis=0).reshape(4, D), jnp.sum(grad_z, axis=0)[None]], axis=0
    )
    lefts = (gqkv_half, gh_half, gu_half, gz_half)
    rights = (ln_one_cut, attended_cut, ln_two_cut, act_cut)

    def rest_cut(left, right, main, rest):
        product = outer_sum(left, right[:, n_shard * main :]).astype(jnp.bfloat16)
        count = product.shape[0] // n_dp
        return jnp.swapaxes(product.reshape(n_dp, count, n_shard, rest), 1, 2)

    def fill(packed_rest, count):
        return jnp.pad(
            packed_rest, ((0, 0), (0, 0), (0, count - packed_rest.shape[2]), (0, 0))
        )

    outgoing = cut_tiles(
        lefts,
        rights,
        plan,
        [
            fill(
                rest_of(
                    jnp.concatenate(
                        [
                            rest_cut(left, right, main_own, rest_own)
                            for left, right in zip(lefts[:3], rights[:3])
                        ],
                        axis=2,
                    )
                ),
                sizes[4],
            ),
            fill(rest_of(rest_cut(gz_half, act_cut, main_proj, rest_proj)), sizes[5]),
        ],
        starts[4:6],
        starts[6],
    ).reshape(n_dp * n_shard, starts[6], LANES)
    summed = lax.psum_scatter(outgoing, axes, scatter_dimension=0, tiled=False).astype(
        jnp.float32
    )

    def owned(start, count, main, rest):
        blocks = main // LANES
        cuts = [summed[start + i * count : start + (i + 1) * count] for i in range(blocks)]
        return jnp.concatenate(cuts + [rest], axis=1).T

    sum_rest = rest_back(
        summed[starts[4] : starts[4] + rest_rows(col_sum, rest_own)], col_sum, rest_own
    )
    grad_qkv = owned(starts[0], cols_qkv, main_own, sum_rest[:cols_qkv])
    grad_attn_out = owned(
        starts[1], cols_out, main_own, sum_rest[cols_qkv : cols_qkv + cols_out]
    )
    grad_fc = owned(starts[2], cols_fc, main_own, sum_rest[cols_qkv + cols_out :])
    grad_proj = owned(
        starts[3],
        cols_proj,
        main_proj,
        rest_back(
            summed[starts[5] : starts[5] + rest_rows(cols_proj, rest_proj)], cols_proj, rest_proj
        ),
    )
    small_total = lax.psum(small_grad.astype(jnp.bfloat16).astype(jnp.float32), axes)
    grad_small = lax.dynamic_slice_in_dim(
        small_total, shard_index * rows_own, rows_own, axis=1
    )
    upd_qkv = adam_update(w_qkv, moment_qkv, second_qkv, grad_qkv, WEIGHT_DECAY)
    upd_out = adam_update(w_attn_out, moment_attn_out, second_attn_out, grad_attn_out, WEIGHT_DECAY)
    upd_fc = adam_update(w_fc, moment_fc, second_fc, grad_fc, WEIGHT_DECAY)
    upd_proj = adam_update(w_proj, moment_proj, second_proj, grad_proj, WEIGHT_DECAY)
    upd_small = adam_update(small_w, moment_small, second_small, grad_small, 0.0)
    return (
        out_act,
        grad_input,
        grad_qkv,
        grad_attn_out,
        grad_fc,
        grad_proj,
        grad_small,
        upd_qkv[0],
        upd_out[0],
        upd_fc[0],
        upd_proj[0],
        upd_small[0],
        upd_qkv[1],
        upd_out[1],
        upd_fc[1],
        upd_proj[1],
        upd_small[1],
        upd_qkv[2],
        upd_out[2],
        upd_fc[2],
        upd_proj[2],
        upd_small[2],
    )


def solution(mesh):
    return jax.shard_map(
        on_device,
        mesh=mesh,
        in_specs=(
            P(("dp", "shard"), None),
            P(("dp", "shard"), None),
            P("dp"),
            P("shard", "dp"),
            P("shard", "dp"),
            P("shard", "dp"),
            P("shard", "dp"),
            P(None, "shard"),
            P("shard", "dp"),
            P("shard", "dp"),
            P("shard", "dp"),
            P("shard", "dp"),
            P(None, "shard"),
            P("shard", "dp"),
            P("shard", "dp"),
            P("shard", "dp"),
            P("shard", "dp"),
            P(None, "shard"),
        ),
        out_specs=(
            P(("dp", "shard"), None),
            P(("dp", "shard"), None),
            P("shard", "dp"),
            P("shard", "dp"),
            P("shard", "dp"),
            P("shard", "dp"),
            P(None, "shard"),
            P("shard", "dp"),
            P("shard", "dp"),
            P("shard", "dp"),
            P("shard", "dp"),
            P(None, "shard"),
            P("shard", "dp"),
            P("shard", "dp"),
            P("shard", "dp"),
            P("shard", "dp"),
            P(None, "shard"),
            P("shard", "dp"),
            P("shard", "dp"),
            P("shard", "dp"),
            P("shard", "dp"),
            P(None, "shard"),
        ),
        check_vma=False,
    )
```

profile of v0, /device:TPU:14, one launch (start us, length us, event | category | flops | bytes accessed | tf_op | source)
XLA Modules:
  0.0 767.8 jit_solution(9073127059171599311)
XLA Ops:
  10.7 2.4 concatenate.71
  15.1 168.8 %all-gather.6.cloned.1.call-done = bf16[112128,128]{1,0:T(8,128)(2,1)} async-done(((bf16[3504,128]{1,0:T(8,128)(2,1)}), bf16[112128,128]{1,0:T(8,128)(2,1)}) %all-gather.6.cloned.1.call-update) | async-done | bytes 28704784 | tf_op jit(solution)/shard_map/all_gather | solution.py:318
  186.7 2.3 copy.583
  189.0 3.7 reshape.359
  209.5 18.5 %shard_map.345 = (bf16[8,408,1088]{2,1,0:T(8,128)(2,1)S(1)}, bf16[8,136,1088]{2,1,0:T(8,128)(2,1)S(1)}, bf16[8,544,1088]{2,1,0:T(8,128)(2,1)}, bf16[8,136,4352]{2,1,0:T(8,128)(2,1)}) custom-call(bf16[8,4,3504,128]{3,2,1,0:T(8,128)(2,1)} %bitcast.228, bf16[8,408,64]{2,1,0:T(8,128)(2,1)S(1)} %copy.673.refs_1_, bf16[8,136,64]{2,1,0:T(8,128)(2,1)S(1)} %copy-done.12, ...), custom_call_target="tpu_custom_call" | custom-call | tf_op jit(solution)/shard_map/pallas_call | solution.py:212
  228.1 3.0 copy-done
  232.1 5.4 fusion.1
  245.4 6.0 fusion.109
  253.4 3.6 concatenate.77
  257.0 6.0 all-gather.4.cloned.1.call-done
  263.1 3.1 fusion.122
  266.1 6.2 fusion.3
  272.3 3.5 convolution_convert_fusion.7
  282.9 11.9 %fusion.117 = (bf16[4352]{0:T(1024)(128)(2,1)}, bf16[128,4352]{1,0:T(8,128)(2,1)S(1)}, bf16[128,4352]{1,0:T(8,128)(2,1)}) fusion(f32[128,4352]{1,0:T(8,128)} %concatenate.77, f32[4352]{0:T(1024)S(1)} %copy-done.88, bf16[128,1088]{1,0:T(8,128)(2,1)S(1)} %concatenate.75.refs_6_, bf16[4352,1088]{1,0:T(8,128)(2,1)} %bitcast.229), kind=kOutput, calls=%fused_computation.224 | convolution fusion | flops 1255042816 | bytes 14231040 | tf_op jit(solution)/shard_map/dot_general | solution.py:32
  294.9 5.9 fusion.103
  302.3 2.2 concatenate.78
  306.5 2.7 fusion.50
  310.5 2.8 convolution_convert_fusion.5
  313.4 3.2 multiply_convert_fusion
  318.5 2.5 copy.668
  334.1 2.4 fusion.124
  336.5 2.2 concatenate.76.refs_7_
  338.8 3.5 fusion.129
  342.3 11.0 %reduce-scatter.8.cloned.1.call-done = bf16[128,2176]{1,0:T(8,128)(2,1)} async-done(((bf16[512,2176]{1,0:T(8,128)(2,1)}), bf16[128,2176]{1,0:T(8,128)(2,1)}) %reduce-scatter.8.cloned.1.call-update) | async-done | bytes 557072
  354.7 2.4 convolution_convert_fusion.1
  358.1 4.5 fusion.111
  364.1 2.2 reshape.376
  367.2 2.8 concatenate.86
  370.1 3.7 reshape.379
  373.7 3.6 copy.624
  377.4 3.0 copy.629.refs_8_
  380.4 2.1 concatenate.82
  384.6 2.9 convert_bitcast_fusion.4
  396.3 12.7 %shard_map.346 = bf16[8,4,3472,128]{3,2,1,0:T(8,128)(2,1)} custom-call(bf16[8,408,128]{2,1,0:T(8,128)(2,1)S(1)} %bitcast.219, bf16[8,136,128]{2,1,0:T(8,128)(2,1)S(1)} %bitcast.221, bf16[8,544,128]{2,1,0:T(8,128)(2,1)S(1)} %bitcast.218, bf16[8,136,128]{2,1,0:T(8,128)(2,1)S(1)} %bitcast.220, bf16[128,1088]{1,0:T(8,128)(2,1)S(1)} %copy-done.4, ...), custom_call_target="tpu_custom_call" | custom-call | tf_op jit(solution)/shard_map/pallas_call | solution.py:251
  411.5 2.4 copy.642
  413.9 2.4 copy.643
  417.4 2.1 copy.639
  420.0 7.9 %fusion.11 = bf16[128,1088]{1,0:T(8,128)(2,1)} fusion(f32[128,1088]{1,0:T(8,128)S(1)} %copy-done.15, bf16[128,4352]{1,0:T(8,128)(2,1)S(1)} %concatenate.76.refs_7_, bf16[1088,4352]{1,0:T(8,128)(2,1)} %bitcast.224, f32[1088]{0:T(1024)S(1)} %add.216), kind=kOutput, calls=%fused_computation.21 | convolution fusion | flops 1212571648 | bytes 11424000 | tf_op jit(solution)/shard_map/dot_general | solution.py:32
  431.0 47.4 %psum.7 = f32[12,1088]{1,0:T(8,128)S(1)} all-reduce(bf16[12,1088]{1,0:T(8,128)(2,1)S(1)} %concatenate.92), channel_id=1, replica_groups=mesh['dp'=8,'shard'=4] {'dp','shard'}, use_global_device_ids=true, to_apply=%region_21.22 | all-reduce | flops 13056 | bytes 78336 | tf_op jit(solution)/shard_map/psum | solution.py:498
  479.1 241.4 %reduce-scatter.10.cloned.1.call-done = bf16[1,3472,128]{2,1,0:T(8,128)(2,1)} async-done(((bf16[32,3472,128]{2,1,0:T(8,128)(2,1)}), bf16[1,3472,128]{2,1,0:T(8,128)(2,1)}) %reduce-scatter.10.cloned.1.call-update) | async-done | bytes 888848
  728.3 3.5 multiply_subtract_fusion
  731.8 2.4 copy.651
  734.2 2.3 copy.653
  739.6 3.2 multiply_subtract_fusion.2
  742.9 2.1 copy.650
  745.0 2.1 copy.652
  754.7 2.1 copy.648
  757.0 2.9 multiply_subtract_fusion.1
  (390 shorter events, 105.1 us)
Async XLA Ops:
  7.2 176.7 %all-gather.6.cloned.1.call-start = ((), (), s32[]{:S(2)}) async-start(), calls=%async_computation.3 | async-start | bytes 29601792 | tf_op jit(solution)/shard_map/all_gather | solution.py:318
  14.4 248.6 %all-gather.4.cloned.1.call-start = ((), (), s32[]{:S(2)}) async-start(), calls=%async_computation.2 | async-start | bytes 2785280 | tf_op jit(solution)/shard_map/all_gather | solution.py:379
  14.7 182.2 %copy-start.19 = (bf16[128,1088]{1,0:T(8,128)(2,1)}, bf16[128,1088]{1,0:T(8,128)(2,1)S(1)}, u32[]{:S(2)}) copy-start(bf16[128,1088]{1,0:T(8,128)(2,1)S(1)} %copy.574) | copy-start | bytes 835588
  14.9 182.1 %copy-start.97 = (f32[128]{0:T(128)}, f32[128]{0:T(128)S(1)}, u32[]{:S(2)}) copy-start(f32[128]{0:T(128)S(1)} %broadcast_multiply_fusion.5) | copy-start | bytes 1540
  15.1 181.9 %copy-start.99 = (f32[128]{0:T(128)}, f32[128]{0:T(128)S(1)}, u32[]{:S(2)}) copy-start(f32[128]{0:T(128)S(1)} %add_rsqrt_fusion.1) | copy-start | bytes 1540
  194.0 6.2 copy-start.37
  198.0 33.1 %copy-start.72 = (bf16[128,16]{1,0:T(8,128)(2,1)}, bf16[128,16]{1,0:T(8,128)(2,1)S(1)}, u32[]{:S(2)}) copy-start(bf16[128,16]{1,0:T(8,128)(2,1)S(1)} %get-tuple-element.312) | copy-start | bytes 12292
  232.1 5.4 copy-start.3
  232.1 7.7 %copy-start.65 = (bf16[128,1088]{0,1:T(8,128)(2,1)S(1)}, bf16[128,1088]{0,1:T(8,128)(2,1)}, u32[]{:S(2)}) copy-start(bf16[128,1088]{0,1:T(8,128)(2,1)} %param.19) | copy-start | bytes 835588
  238.4 4.9 copy-start.86
  238.4 5.6 copy-start.85
  239.3 113.9 %reduce-scatter.8.cloned.1.call-start = ((), (), s32[]{:S(2)}) async-start(), calls=%async_computation.4 | async-start | bytes 2785280
  240.1 11.4 %copy-start.25 = (bf16[128,1088]{1,0:T(8,128)(2,1)}, bf16[128,1088]{1,0:T(8,128)(2,1)S(1)}, u32[]{:S(2)}) copy-start(bf16[128,1088]{1,0:T(8,128)(2,1)S(1)} %copy.601) | copy-start | bytes 835588
  240.2 11.3 %copy-start.94 = (f32[128]{0:T(128)}, f32[128]{0:T(128)S(1)}, u32[]{:S(2)}) copy-start(f32[128]{0:T(128)S(1)} %get-tuple-element.243) | copy-start | bytes 1540
  257.0 9.1 %copy-start.40 = (bf16[128,1088]{0,1:T(8,128)(2,1)S(1)}, bf16[128,1088]{0,1:T(8,128)(2,1)}, u32[]{:S(2)}) copy-start(bf16[128,1088]{0,1:T(8,128)(2,1)} %slice.634) | copy-start | bytes 835588
  257.0 9.1 %copy-start.79 = (pred[128,512]{1,0:T(8,128)(4,1)S(1)}, pred[128,512]{1,0:T(8,128)(4,1)}, u32[]{:S(2)}) copy-start(pred[128,512]{1,0:T(8,128)(4,1)} %fusion.55) | copy-start | bytes 196612
  272.3 5.8 copy-start.81
  280.1 26.4 %copy-start.14 = (f32[128,1088]{1,0:T(8,128)}, f32[128,1088]{1,0:T(8,128)S(1)}, u32[]{:S(2)}) copy-start(f32[128,1088]{1,0:T(8,128)S(1)} %get-tuple-element.333) | copy-start | bytes 1671172
  281.8 13.1 %copy-start.48 = (bf16[128,16]{1,0:T(8,128)(2,1)}, bf16[128,16]{1,0:T(8,128)(2,1)S(1)}, u32[]{:S(2)}) copy-start(bf16[128,16]{1,0:T(8,128)(2,1)S(1)} %get-tuple-element.305) | copy-start | bytes 12292
  281.8 13.0 %copy-start.50 = (bf16[128,16]{1,0:T(8,128)(2,1)}, bf16[128,16]{1,0:T(8,128)(2,1)S(1)}, u32[]{:S(2)}) copy-start(bf16[128,16]{1,0:T(8,128)(2,1)S(1)} %get-tuple-element.306) | copy-start | bytes 12292
  281.8 13.0 %copy-start.52 = (bf16[128,16]{1,0:T(8,128)(2,1)}, bf16[128,16]{1,0:T(8,128)(2,1)S(1)}, u32[]{:S(2)}) copy-start(bf16[128,16]{1,0:T(8,128)(2,1)S(1)} %get-tuple-element.307) | copy-start | bytes 12292
  282.9 12.0 %copy-start.9 = (bf16[128,1088]{1,0:T(8,128)(2,1)}, bf16[128,1088]{1,0:T(8,128)(2,1)S(1)}, u32[]{:S(2)}) copy-start(bf16[128,1088]{1,0:T(8,128)(2,1)S(1)} %concatenate.75.refs_6_) | copy-start | bytes 835588
  294.9 5.9 copy-start.17
  300.8 5.7 copy-start.26
  321.1 399.5 %reduce-scatter.10.cloned.1.call-start = ((), (), s32[]{:S(2)}) async-start(), calls=%async_computation.5 | async-start | bytes 29331456
  334.1 4.7 copy-start.27
  338.8 15.8 %copy-start.73 = (bf16[128,16]{1,0:T(8,128)(2,1)S(1)}, bf16[128,16]{1,0:T(8,128)(2,1)}, u32[]{:S(2)}) copy-start(bf16[128,16]{1,0:T(8,128)(2,1)} %copy-done.72) | copy-start | bytes 12292
  338.8 15.8 %copy-start.74 = (bf16[128,16]{1,0:T(8,128)(2,1)S(1)}, bf16[128,16]{1,0:T(8,128)(2,1)}, u32[]{:S(2)}) copy-start(bf16[128,16]{1,0:T(8,128)(2,1)} %get-tuple-element.313) | copy-start | bytes 12292
  338.8 15.8 %copy-start.75 = (bf16[128,16]{1,0:T(8,128)(2,1)S(1)}, bf16[128,16]{1,0:T(8,128)(2,1)}, u32[]{:S(2)}) copy-start(bf16[128,16]{1,0:T(8,128)(2,1)} %get-tuple-element.314) | copy-start | bytes 12292
  338.8 15.8 %copy-start.76 = (bf16[128,16]{1,0:T(8,128)(2,1)S(1)}, bf16[128,16]{1,0:T(8,128)(2,1)}, u32[]{:S(2)}) copy-start(bf16[128,16]{1,0:T(8,128)(2,1)} %get-tuple-element.315) | copy-start | bytes 12292
  342.3 14.8 %copy-start.31 = (bf16[128,17,64]{0,2,1:T(8,128)(2,1)S(1)}, bf16[128,17,64]{0,2,1:T(8,128)(2,1)}, u32[]{:S(2)}) copy-start(bf16[128,17,64]{0,2,1:T(8,128)(2,1)} %get-tuple-element.289) | copy-start | bytes 835588
  354.6 7.9 %copy-start.23 = (bf16[128,2176]{0,1:T(8,128)(2,1)}, bf16[128,2176]{0,1:T(8,128)(2,1)S(1)}, u32[]{:S(2)}) copy-start(bf16[128,2176]{0,1:T(8,128)(2,1)S(1)} %copy.669) | copy-start | bytes 1671172
  377.4 5.2 copy-start.70
  411.5 4.8 copy-start.47
  413.9 5.6 copy-start.84
  413.9 5.8 copy-start.92
  413.9 5.8 copy-start.91
  413.9 5.8 copy-start.90
  413.9 5.8 copy-start.89
  413.9 5.9 copy-start.96
  413.9 5.9 copy-start.15
  419.9 9.8 %copy-start.93 = (bf16[1088]{0:T(1024)(128)(2,1)S(1)}, bf16[1088]{0:T(1024)(128)(2,1)}, u32[]{:S(2)}) copy-start(bf16[1088]{0:T(1024)(128)(2,1)} %get-tuple-element.208) | copy-start | bytes 6532
  419.9 9.8 %copy-start.24 = (bf16[128,2176]{0,1:T(8,128)(2,1)S(1)}, bf16[128,2176]{0,1:T(8,128)(2,1)}, u32[]{:S(2)}) copy-start(bf16[128,2176]{0,1:T(8,128)(2,1)} %copy-done.23) | copy-start | bytes 1671172
  419.9 10.0 %copy-start.39 = (bf16[128,1088]{1,0:T(8,128)(2,1)S(1)}, bf16[128,1088]{1,0:T(8,128)(2,1)}, u32[]{:S(2)}) copy-start(bf16[128,1088]{1,0:T(8,128)(2,1)} %get-tuple-element.271) | copy-start | bytes 835588
  419.9 58.5 %copy-start.78 = (f32[12,272]{1,0:T(8,128)S(1)}, f32[12,272]{1,0:T(8,128)}, u32[]{:S(2)}) copy-start(f32[12,272]{1,0:T(8,128)} %param.25) | copy-start | bytes 39172
  419.9 58.5 %copy-start.82 = (f32[12,272]{1,0:T(8,128)S(1)}, f32[12,272]{1,0:T(8,128)}, u32[]{:S(2)}) copy-start(f32[12,272]{1,0:T(8,128)} %param.30) | copy-start | bytes 39172
  419.9 58.5 %copy-start.83 = (f32[12,272]{1,0:T(8,128)S(1)}, f32[12,272]{1,0:T(8,128)}, u32[]{:S(2)}) copy-start(f32[12,272]{1,0:T(8,128)} %param.35) | copy-start | bytes 39172
  748.2 8.7 %copy-start.35 = (f32[1088,136]{0,1:T(8,128)S(1)}, f32[1088,136]{0,1:T(8,128)}, u32[]{:S(2)}) copy-start(f32[1088,136]{0,1:T(8,128)} %param.24) | copy-start | bytes 1775620
  (58 other events, 129.2 us)
Sparse Core Ops, SparseCore 0:
  14.6 169.2 all-gather.5
  239.4 23.5 all-gather.3
  321.2 31.9 reduce-scatter.7
  409.2 311.3 reduce-scatter.9
where the time goes:
time: 778 us; the launch traced here: 768 us
  waiting for transfers between devices  427 us (55%)
  local copies, waits for them, and re-layouts  147 us (19%)
  matrix products  67.7 us (9%)
  blocking collectives  47.4 us (6%)
  Pallas kernels  31.2 us (4%)
  other arithmetic  30.9 us (4%)
  between operations  15.8 us (2%)
    unnamed x6, waiting for transfers between devices  252 us
    all_gather x1, waiting for transfers between devices, on_device(): lax.all_gather(packed, axes, axis=0, tiled=False)  169 us
    unnamed x254, local copies, waits for them, and re-layouts  59 us
    psum x1, blocking collectives, on_device(): lax.psum(small_grad.astype(jnp.bfloat16).astype(jnp.float32), axes)  47.4 us
    dot_general x4, matrix products, back_product(): lax.dot_general(left_rows, right_rows, (((1,), (1,)), ((), ())), preferre...  27.1 us
    pallas_call x1, Pallas kernels, join_tiles(): pl.pallas_call(lambda *refs: join_kernel(plan, *refs), grid=(n_dp,), in_s...  18.5 us
    dot_general x4, matrix products, matmul(): return jnp.dot(left_rows, right_rows, preferred_element_type=jnp.float32)  17.4 us
  transfers between devices with their start and end apart: 4, of which 4 were waited for; matrix products, arithmetic and copies ran while one was open for 8% of the time, Pallas kernels for 0%

commit v1 on v0

--- a/solution.py
+++ b/solution.py
@@ -260,7 +260,7 @@
     )(*lefts, *right_list, *rest_list)
 
 
-def on_device(
+def on_device_general(
     tokens_in,
     cotangent,
     segment_ids,
@@ -530,6 +530,809 @@
     )
 
 
+AXES = ("dp", "shard")
+MESH_ID = pl.DeviceIdType.MESH
+COLS = 2
+PIECES = 3
+
+
+def place():
+    d = lax.axis_index("dp")
+    s = lax.axis_index("shard")
+    z, y = d // COLS, d % COLS
+    x, c = s // 2, s % 2
+    x_dev = (d, (1 - x) * 2 + c)
+    y_dev = (z * COLS + 1 - y, s)
+    near = tuple(a * (1 - c) + b * c for a, b in zip(x_dev, y_dev))
+    far = tuple(b * (1 - c) + a * c for a, b in zip(x_dev, y_dev))
+    up = (d + COLS, s)
+    down = (d - COLS, s)
+    sib = (d, x * 2 + 1 - c)
+    return d, s, z, y, x, c, near, far, up, down, sib
+
+
+def flip(value, change):
+    return value + change - 2 * value * change
+
+
+def enter(n_dp, n_shard, d, s):
+    barrier = pltpu.get_barrier_semaphore()
+    for step in range(1, n_dp):
+        pl.semaphore_signal(
+            barrier, inc=1, device_id=((d + step) % n_dp, s), device_id_type=MESH_ID
+        )
+    for step in range(1, n_shard):
+        pl.semaphore_signal(
+            barrier, inc=1, device_id=(d, (s + step) % n_shard), device_id_type=MESH_ID
+        )
+    pl.semaphore_wait(barrier, n_dp + n_shard - 2)
+
+
+def gather_kernel(
+    n_dp,
+    n_shard,
+    cut_ref,
+    proj_ref,
+    small_ref,
+    full_ref,
+    small_out,
+    own,
+    swap,
+    local_sem,
+    swap_sem,
+    small_sem,
+    send_sem,
+    recv_sem,
+    sib_sem,
+):
+    d, s, z, y, x, c, near, far, up, down, sib = place()
+    depth = n_dp // COLS
+    lanes = cut_ref.shape[-1]
+
+    def where(zs, fa, fb):
+        fx = fa * (1 - c) + fb * c
+        fy = fb * (1 - c) + fa * c
+        return zs * COLS + flip(y, fy), flip(x, fx) * 2 + c
+
+    def number(zs, fa, fb, k):
+        return ((zs * 2 + fa) * 2 + fb) * PIECES + k
+
+    def copy(kind, zs, fa, fb, k, src=None):
+        dp, sh = where(zs, fa, fb)
+        block = full_ref.at[dp, sh, k]
+        target = (near, far, up, down, sib)[kind]
+        mine = number(zs, fa, fb, k)
+        if kind == 4:
+            arrive = sib_sem.at[mine]
+        else:
+            arrive = recv_sem.at[number(zs, 1 if kind == 0 else fa, 1 if kind == 1 else fb, k)]
+        return pltpu.make_async_remote_copy(
+            src_ref=block if src is None else src,
+            dst_ref=block,
+            send_sem=send_sem.at[kind, mine],
+            recv_sem=arrive,
+            device_id=target,
+            device_id_type=MESH_ID,
+        )
+
+    def arrived(zs, fa, fb, k):
+        dp, sh = where(zs, fa, fb)
+        block = full_ref.at[dp, sh, k]
+        pltpu.make_async_copy(block, block, recv_sem.at[number(zs, fa, fb, k)]).wait()
+
+    enter(n_dp, n_shard, d, s)
+
+    def swap_copy(step):
+        peer = (s + step) % n_shard
+        return pltpu.make_async_remote_copy(
+            src_ref=cut_ref.at[peer],
+            dst_ref=swap.at[s],
+            send_sem=swap_sem.at[0, step],
+            recv_sem=swap_sem.at[1, step],
+            device_id=(d, peer),
+            device_id_type=MESH_ID,
+        )
+
+    def small_copy(step):
+        peer = (s + step) % n_shard
+        return pltpu.make_async_remote_copy(
+            src_ref=small_ref,
+            dst_ref=small_out.at[s],
+            send_sem=small_sem.at[0, step],
+            recv_sem=small_sem.at[1, step],
+            device_id=(d, peer),
+            device_id_type=MESH_ID,
+        )
+
+    for step in range(1, n_shard):
+        swap_copy(step).start()
+    own_cut = pltpu.make_async_copy(cut_ref.at[s], swap.at[s], local_sem.at[0])
+    own_cut.start()
+    own_small = pltpu.make_async_copy(small_ref, small_out.at[s], local_sem.at[1])
+    own_small.start()
+
+    def spread(k, src):
+        copy(0, z, 0, 0, k, src).start()
+        copy(1, z, 0, 0, k, src).start()
+
+        @pl.when(z < depth - 1)
+        def _():
+            copy(2, z, 0, 0, k, src).start()
+
+        @pl.when(z > 0)
+        def _():
+            copy(3, z, 0, 0, k, src).start()
+
+        copy(4, z, 0, 0, k, src).start()
+        keep = pltpu.make_async_copy(src, full_ref.at[d, s, k], local_sem.at[2 + k])
+        keep.start()
+
+    spread(2, proj_ref)
+    for step in range(1, n_shard):
+        small_copy(step).start()
+    own_cut.wait()
+    for step in range(1, n_shard):
+        swap_copy(step).wait()
+    for k in (1, 0):
+        for part in range(n_shard):
+            own[k, :, part * lanes : (part + 1) * lanes] = swap[part, k]
+    spread(1, own.at[1])
+    spread(0, own.at[0])
+
+    def pass_on(zs, fa, k, go_up, go_down, go_near):
+        arrived(zs, fa, 0, k)
+        if go_up:
+
+            @pl.when(z < depth - 1)
+            def _():
+                copy(2, zs, fa, 0, k).start()
+
+        if go_down:
+
+            @pl.when(z > 0)
+            def _():
+                copy(3, zs, fa, 0, k).start()
+
+        if go_near:
+            copy(0, zs, fa, 0, k).start()
+        copy(1, zs, fa, 0, k).start()
+        copy(4, zs, fa, 0, k).start()
+
+    def from_near(zs):
+        pass_on(zs, 1, 0, False, False, False)
+
+    def from_far(zs):
+        def step(j, carry):
+            fa, k = j // PIECES, PIECES - 1 - j % PIECES
+            arrived(zs, fa, 1, k)
+            copy(4, zs, fa, 1, k).start()
+            return carry
+
+        lax.fori_loop(0, 2 * PIECES, step, 0)
+
+    pass_on(z, 1, 2, True, True, False)
+    pass_on(z, 1, 1, True, True, False)
+    from_near(z)
+    for delta in range(1, depth):
+        for sign in (-1, 1):
+            zs = z + sign * delta
+
+            @pl.when((zs >= 0) & (zs < depth))
+            def _():
+                for k, fa in ((2, 0), (1, 0), (0, 0), (2, 1), (1, 1)):
+                    pass_on(zs, fa, k, sign < 0, sign > 0, k == 0)
+
+        for sign in (-1, 1):
+            zs = z + sign * delta
+
+            @pl.when((zs >= 0) & (zs < depth))
+            def _():
+                from_near(zs)
+
+        for sign in (-1, 1) if delta > 1 else (0,):
+            zs = z + sign * (delta - 1)
+
+            @pl.when((zs >= 0) & (zs < depth))
+            def _():
+                from_far(zs)
+
+    for sign in (-1, 1):
+        zs = z + sign * (depth - 1)
+
+        @pl.when((zs >= 0) & (zs < depth))
+        def _():
+            from_far(zs)
+
+    own_small.wait()
+    for k in range(PIECES):
+        pltpu.make_async_copy(own.at[0], full_ref.at[d, s, k], local_sem.at[2 + k]).wait()
+    for step in range(1, n_shard):
+        small_copy(step).wait()
+
+    def finish(zs, carry):
+        for fa in range(2):
+            for k in range(PIECES):
+                if k > 0 or fa == 0:
+
+                    @pl.when((z < depth - 1) & (zs <= z))
+                    def _():
+                        copy(2, zs, fa, 0, k).wait_send()
+
+                    @pl.when((z > 0) & (zs >= z))
+                    def _():
+                        copy(3, zs, fa, 0, k).wait_send()
+
+                if fa == 0:
+                    if k == 0:
+                        copy(0, zs, fa, 0, k).wait_send()
+                    else:
+
+                        @pl.when(zs == z)
+                        def _():
+                            copy(0, zs, fa, 0, k).wait_send()
+
+                copy(1, zs, fa, 0, k).wait_send()
+                for fb in range(2):
+                    copy(4, zs, fa, fb, k).wait()
+        return carry
+
+    lax.fori_loop(0, depth, finish, 0)
+
+
+def gather_rows(cut, proj, small, n_dp, n_shard):
+    piece_rows, width = proj.shape
+    count = n_dp // COLS * 4 * PIECES
+    shape = (n_dp, n_shard, PIECES, piece_rows, width)
+    return pl.pallas_call(
+        lambda *refs: gather_kernel(n_dp, n_shard, *refs),
+        out_shape=[
+            jax.ShapeDtypeStruct(shape, cut.dtype),
+            jax.ShapeDtypeStruct((n_shard,) + small.shape, small.dtype),
+        ],
+        in_specs=[pl.BlockSpec(memory_space=pltpu.VMEM)] * 3,
+        out_specs=[
+            pl.BlockSpec(memory_space=pltpu.HBM),
+            pl.BlockSpec(memory_space=pltpu.VMEM),
+        ],
+        scratch_shapes=[
+            pltpu.VMEM((PIECES - 1, piece_rows, width), cut.dtype),
+            pltpu.VMEM(cut.shape, cut.dtype),
+            pltpu.SemaphoreType.DMA((2 + PIECES,)),
+            pltpu.SemaphoreType.DMA((2, n_shard)),
+            pltpu.SemaphoreType.DMA((2, n_shard)),
+            pltpu.SemaphoreType.DMA((5, count)),
+            pltpu.SemaphoreType.DMA((count,)),
+            pltpu.SemaphoreType.DMA((count,)),
+        ],
+        compiler_params=pltpu.CompilerParams(
+            collective_id=0, has_side_effects=True, vmem_limit_bytes=24 * 1024 * 1024
+        ),
+    )(cut, proj, small)
+
+
+def reduce_kernel(
+    n_dp,
+    n_shard,
+    grad_ref,
+    small_ref,
+    swap_out,
+    proj_out,
+    small_out,
+    total,
+    from_sib,
+    from_far,
+    from_near,
+    from_line,
+    cut,
+    small_part,
+    small_sum,
+    small_all,
+    local_sem,
+    sib_sem,
+    far_sem,
+    near_sem,
+    line_sem,
+    swap_sem,
+    small_sem,
+    small_dp_sem,
+    own_sem,
+):
+    d, s, z, y, x, c, near, far, up, down, sib = place()
+    depth = n_dp // COLS
+    lanes = swap_out.shape[-1]
+    per_level = 2 * PIECES
+
+    def where(zq, fa, fb, core):
+        fx = fa * (1 - core) + fb * core
+        fy = fb * (1 - core) + fa * core
+        return zq * COLS + flip(y, fy), flip(x, fx) * 2 + core
+
+    def spot(zq, fa, fb, k):
+        return ((zq * 2 + fb) * 2 + fa) * PIECES + k
+
+    def order(j):
+        level = j // per_level
+        zq = (level % 2) * (depth - 1 - level // 2) + (1 - level % 2) * (level // 2)
+        k = j % per_level // 2
+        fa = 1 - j % 2
+        return zq, fa, k
+
+    def remote(src, dst, sems, number, target):
+        return pltpu.make_async_remote_copy(
+            src_ref=src,
+            dst_ref=dst,
+            send_sem=sems.at[0, number],
+            recv_sem=sems.at[1, number],
+            device_id=target,
+            device_id_type=MESH_ID,
+        )
+
+    def sib_copy(zq, fa, fb, k):
+        dp, sh = where(zq, fa, fb, 1 - c)
+        slot = spot(zq, fa, fb, k)
+        return remote(grad_ref.at[dp, sh, k], from_sib.at[slot], sib_sem, slot, sib)
+
+    def own_copy(zq, fa, fb, k):
+        dp, sh = where(zq, fa, fb, c)
+        slot = spot(zq, fa, fb, k)
+        return pltpu.make_async_copy(grad_ref.at[dp, sh, k], total.at[slot], local_sem.at[slot])
+
+    def far_copy(zq, fa, k):
+        slot = (zq * 2 + fa) * PIECES + k
+        return remote(total.at[spot(zq, fa, 1, k)], from_far.at[slot], far_sem, slot, far)
+
+    def near_copy(zq, k, slot):
+        return remote(total.at[spot(zq, 1, 0, k)], from_near.at[slot], near_sem, slot, near)
+
+    def line_copy(way, zq, fa, k):
+        slot = (way * depth + zq) * 5 + (0 if k == 0 else 2 * k - 1 + fa)
+        return remote(
+            total.at[spot(zq, fa, 0, k)],
+            from_line.at[slot],
+            line_sem,
+            slot,
+            (up, down)[way],
+        )
+
+    def add(slot, other):
+        total[slot] = (
+            total[slot].astype(jnp.float32) + other[...].astype(jnp.float32)
+        ).astype(total.dtype)
+
+    enter(n_dp, n_shard, d, s)
+
+    def small_shard(step):
+        peer = (s + step) % n_shard
+        return remote(small_ref.at[peer], small_part.at[s], small_sem, step, (d, peer))
+
+    for step in range(1, n_shard):
+        small_shard(step).start()
+    own_small = pltpu.make_async_copy(small_ref.at[s], small_part.at[s], own_sem.at[0])
+    own_small.start()
+
+    def begin(fb):
+        def step(j, carry):
+            zq, fa, k = order(j)
+            sib_copy(zq, fa, fb, k).start()
+            own_copy(zq, fa, fb, k).start()
+            return carry
+
+        return step
+
+    lax.fori_loop(0, depth * per_level, begin(1), 0)
+    lax.fori_loop(0, depth * per_level, begin(0), 0)
+
+    def merge(fb):
+        def step(j, carry):
+            zq, fa, k = order(j)
+            own_copy(zq, fa, fb, k).wait()
+            sib_copy(zq, fa, fb, k).wait_recv()
+            slot = spot(zq, fa, fb, k)
+            add(slot, from_sib.at[slot])
+            if fb == 1:
+                far_copy(zq, fa, k).start()
+            return carry
+
+        return step
+
+    lax.fori_loop(0, depth * per_level, merge(1), 0)
+
+    own_small.wait()
+    for step in range(1, n_shard):
+        small_shard(step).wait()
+    small_sum[...] = jnp.sum(small_part[...], axis=0)
+
+    def small_dp(step):
+        peer = (d + step) % n_dp
+        return remote(small_sum, small_all.at[d], small_dp_sem, step, (peer, s))
+
+    lax.fori_loop(0, depth * per_level, merge(0), 0)
+    for step in range(1, n_dp):
+        small_dp(step).start()
+    own_all = pltpu.make_async_copy(small_sum, small_all.at[d], own_sem.at[1])
+    own_all.start()
+
+    def level_step(level, carry):
+        zq = (level % 2) * (depth - 1 - level // 2) + (1 - level % 2) * (level // 2)
+
+        def line_step(fa, k):
+            @pl.when(zq < z)
+            def _():
+                @pl.when(z < depth - 1)
+                def _():
+                    line_copy(1, zq, fa, k).wait_recv()
+                    add(spot(zq, fa, 0, k), from_line.at[(depth + zq) * 5 + slot_of(fa, k)])
+
+                line_copy(1, zq, fa, k).start()
+
+            @pl.when(zq > z)
+            def _():
+                @pl.when(z > 0)
+                def _():
+                    line_copy(0, zq, fa, k).wait_recv()
+                    add(spot(zq, fa, 0, k), from_line.at[zq * 5 + slot_of(fa, k)])
+
+                line_copy(0, zq, fa, k).start()
+
+        def slot_of(fa, k):
+            return 0 if k == 0 else 2 * k - 1 + fa
+
+        def take_far(fa, k):
+            far_copy(zq, fa, k).wait_recv()
+            add(spot(zq, fa, 0, k), from_far.at[(zq * 2 + fa) * PIECES + k])
+
+        take_far(1, 0)
+        near_copy(zq, 0, zq).start()
+        take_far(0, 0)
+        for k in (1, 2):
+            for fa in (1, 0):
+                take_far(fa, k)
+                line_step(fa, k)
+        near_copy(zq, 0, zq).wait_recv()
+        add(spot(zq, 0, 0, 0), from_near.at[zq])
+        line_step(0, 0)
+        return carry
+
+    lax.fori_loop(0, depth, level_step, 0)
+
+    def last(fa, k):
+        number = 0 if k == 0 else 2 * k - 1 + fa
+
+        @pl.when(z < depth - 1)
+        def _():
+            line_copy(1, z, fa, k).wait_recv()
+            add(spot(z, fa, 0, k), from_line.at[(depth + z) * 5 + number])
+
+        @pl.when(z > 0)
+        def _():
+            line_copy(0, z, fa, k).wait_recv()
+            add(spot(z, fa, 0, k), from_line.at[z * 5 + number])
+
+    for k in (1, 2):
+        last(1, k)
+        near_copy(z, k, depth + k - 1).start()
+    for k in (1, 0, 2):
+        last(0, k)
+        if k > 0:
+            near_copy(z, k, depth + k - 1).wait_recv()
+            add(spot(z, 0, 0, k), from_near.at[depth + k - 1])
+        if k < 2:
+            for part in range(n_shard):
+                cut[part, k] = total[spot(z, 0, 0, k), :, part * lanes : (part + 1) * lanes]
+
+    def swap_copy(step):
+        peer = (s + step) % n_shard
+        return remote(cut.at[peer], swap_out.at[s], swap_sem, step, (d, peer))
+
+    for step in range(1, n_shard):
+        swap_copy(step).start()
+    own_cut = pltpu.make_async_copy(cut.at[s], swap_out.at[s], own_sem.at[2])
+    own_cut.start()
+    proj_out[...] = total[spot(z, 0, 0, 2)]
+    own_all.wait()
+    for step in range(1, n_dp):
+        small_dp(step).wait()
+    small_out[...] = jnp.sum(small_all[...], axis=0)
+    own_cut.wait()
+    for step in range(1, n_shard):
+        swap_copy(step).wait()
+
+    def finish(zq, carry):
+        for k in range(PIECES):
+            for fa in range(2):
+                for fb in range(2):
+                    sib_copy(zq, fa, fb, k).wait_send()
+                far_copy(zq, fa, k).wait_send()
+                if k > 0 or fa == 0:
+
+                    @pl.when(zq < z)
+                    def _():
+                        line_copy(1, zq, fa, k).wait_send()
+
+                    @pl.when(zq > z)
+                    def _():
+                        line_copy(0, zq, fa, k).wait_send()
+
+        near_copy(zq, 0, zq).wait_send()
+        return carry
+
+    lax.fori_loop(0, depth, finish, 0)
+    for k in (1, 2):
+        near_copy(z, k, depth + k - 1).wait_send()
+
+
+def reduce_rows(grads, small, n_dp, n_shard):
+    piece_rows, width = grads.shape[-2:]
+    lanes = width // n_shard
+    depth = n_dp // COLS
+    count = depth * 4 * PIECES
+    kind = grads.dtype
+
+    def pieces(number):
+        return pltpu.VMEM((number, piece_rows, width), kind)
+
+    def sems(*shape):
+        return pltpu.SemaphoreType.DMA(shape)
+
+    return pl.pallas_call(
+        lambda *refs: reduce_kernel(n_dp, n_shard, *refs),
+        out_shape=[
+            jax.ShapeDtypeStruct((n_shard, PIECES - 1, piece_rows, lanes), kind),
+            jax.ShapeDtypeStruct((piece_rows, width), kind),
+            jax.ShapeDtypeStruct(small.shape[1:], small.dtype),
+        ],
+        in_specs=[
+            pl.BlockSpec(memory_space=pltpu.HBM),
+            pl.BlockSpec(memory_space=pltpu.VMEM),
+        ],
+        out_specs=[pl.BlockSpec(memory_space=pltpu.VMEM)] * 3,
+        scratch_shapes=[
+            pieces(count),
+            pieces(count),
+            pieces(depth * 2 * PIECES),
+            pieces(depth + 2),
+            pieces(2 * depth * 5),
+            pltpu.VMEM((n_shard, PIECES - 1, piece_rows, lanes), kind),
+            pltpu.VMEM(small.shape, small.dtype),
+            pltpu.VMEM(small.shape[1:], small.dtype),
+            pltpu.VMEM((n_dp,) + small.shape[1:], small.dtype),
+            sems(count),
+            sems(2, count),
+            sems(2, depth * 2 * PIECES),
+            sems(2, depth + 2),
+            sems(2, 2 * depth * 5),
+            sems(2, n_shard),
+            sems(2, n_shard),
+            sems(2, n_dp),
+            sems(3),
+        ],
+        compiler_params=pltpu.CompilerParams(
+            collective_id=1, has_side_effects=True, vmem_limit_bytes=62 * 1024 * 1024
+        ),
+    )(grads, small)
+
+
+def fits(w_qkv, w_attn_out, w_fc, w_proj, n_dp, n_shard):
+    unit = w_proj.shape[1]
+    return (
+        n_shard == 4
+        and n_dp % COLS == 0
+        and n_dp > COLS
+        and unit % 8 == 0
+        and w_qkv.shape[1] == 3 * unit
+        and w_attn_out.shape[1] == unit
+        and w_fc.shape[1] == 4 * unit
+        and w_proj.shape[0] == w_qkv.shape[0] * n_shard
+    )
+
+
+def on_device(
+    tokens_in,
+    cotangent,
+    segment_ids,
+    w_qkv,
+    w_attn_out,
+    w_fc,
+    w_proj,
+    small_w,
+    moment_qkv,
+    moment_attn_out,
+    moment_fc,
+    moment_proj,
+    moment_small,
+    second_qkv,
+    second_attn_out,
+    second_fc,
+    second_proj,
+    second_small,
+):
+    n_dp = lax.axis_size("dp")
+    n_shard = lax.axis_size("shard")
+    if not fits(w_qkv, w_attn_out, w_fc, w_proj, n_dp, n_shard):
+        return on_device_general(
+            tokens_in,
+            cotangent,
+            segment_ids,
+            w_qkv,
+            w_attn_out,
+            w_fc,
+            w_proj,
+            small_w,
+            moment_qkv,
+            moment_attn_out,
+            moment_fc,
+            moment_proj,
+            moment_small,
+            second_qkv,
+            second_attn_out,
+            second_fc,
+            second_proj,
+            second_small,
+        )
+    rows_own = w_qkv.shape[0]
+    cols_qkv, cols_out = w_qkv.shape[1], w_attn_out.shape[1]
+    unit = w_proj.shape[1]
+    small_count = small_w.shape[0]
+    cut = jnp.concatenate(
+        [w.astype(jnp.bfloat16).T for w in (w_qkv, w_attn_out, w_fc)], axis=0
+    ).reshape(n_shard, PIECES - 1, unit, rows_own)
+    gathered, small_all = gather_rows(
+        cut,
+        w_proj.astype(jnp.bfloat16).T,
+        pad_rows(small_w.astype(jnp.bfloat16), eight(small_count)),
+        n_dp,
+        n_shard,
+    )
+    units = gathered[:, :, : PIECES - 1].reshape(n_dp, n_shard * 2, unit, D)
+    full_qkv = units[:, :3].reshape(3 * D, D)
+    full_out = units[:, 3].reshape(D, D)
+    full_fc = units[:, 4:].reshape(FF, D)
+    full_proj = [gathered[:, t, PIECES - 1].reshape(D, D) for t in range(n_shard)]
+    small_vals = jnp.swapaxes(small_all, 0, 1).reshape(-1, D)[:small_count].astype(jnp.float32)
+    gain_one = small_vals[0]
+    shift_one = small_vals[1]
+    q_bias = small_vals[2]
+    v_bias = small_vals[3]
+    out_bias = small_vals[4]
+    gain_two = small_vals[5]
+    shift_two = small_vals[6]
+    fc_bias = small_vals[7:11].reshape(FF)
+    proj_bias = small_vals[11]
+    tok_rows = tokens_in.shape[0]
+    group_size = segment_ids.shape[0]
+    shard_index = lax.axis_index("shard")
+    own_seg = lax.dynamic_slice_in_dim(segment_ids, shard_index * tok_rows, tok_rows)
+    query_pos = shard_index * tok_rows + jnp.arange(tok_rows, dtype=jnp.int32)
+    x_rows = tokens_in.astype(jnp.float32)
+    normed_one, inv_one, ln_one = norm_forward(x_rows, gain_one, shift_one)
+    ln_one_half = ln_one.astype(jnp.bfloat16)
+    qkv_rows = back_product(ln_one_half, full_qkv) + jnp.concatenate(
+        [q_bias, jnp.zeros_like(q_bias), v_bias]
+    )
+    queries = qkv_rows[:, :D].astype(jnp.bfloat16)
+    kv_half = qkv_rows[:, D:].astype(jnp.bfloat16)
+    kv_all = lax.all_gather(kv_half, "shard", axis=0, tiled=True)
+    key_all = kv_all[:, :D]
+    value_all = kv_all[:, D:]
+    key_pos = jnp.arange(group_size, dtype=jnp.int32)
+    allowed = (
+        (own_seg[:, None] == segment_ids[None, :])
+        & (key_pos[None, :] <= query_pos[:, None])
+        & ((own_seg >= 0)[:, None] | (key_pos[None, :] == query_pos[:, None]))
+    )
+    attended, log_total = attend_forward(queries, key_all, value_all, allowed)
+    resid = x_rows + back_product(attended, full_out) + out_bias
+    normed_two, inv_two, ln_two = norm_forward(resid, gain_two, shift_two)
+    ln_two_half = ln_two.astype(jnp.bfloat16)
+    pre_act = back_product(ln_two_half, full_fc) + fc_bias
+    act_half = jax.nn.gelu(pre_act, approximate=False).astype(jnp.bfloat16)
+    act_parts = [act_half[:, t * D : (t + 1) * D] for t in range(n_shard)]
+    out_sum = resid + proj_bias
+    for act_part, proj_part in zip(act_parts, full_proj):
+        out_sum = out_sum + back_product(act_part, proj_part)
+    out_act = out_sum.astype(jnp.bfloat16)
+    valid = (own_seg >= 0).astype(jnp.float32)
+    grad_z = cotangent.astype(jnp.float32) * valid[:, None]
+    gz_half = grad_z.astype(jnp.bfloat16)
+    d_pre = jnp.concatenate([matmul(gz_half, part) for part in full_proj], axis=1) * gelu_slope(
+        pre_act
+    )
+    gu_half = d_pre.astype(jnp.bfloat16)
+    d_ln_two = matmul(gu_half, full_fc)
+    d_resid = grad_z + norm_backward(d_ln_two, normed_two, inv_two, gain_two)
+    gh_half = d_resid.astype(jnp.bfloat16)
+    grad_attn = matmul(gh_half, full_out).astype(jnp.bfloat16)
+    d_query, d_keys_all, d_values_all = attend_backward(
+        queries, key_all, value_all, allowed, log_total, attended, grad_attn
+    )
+    d_kv = lax.psum_scatter(
+        jnp.concatenate(
+            [d_keys_all.astype(jnp.bfloat16), d_values_all.astype(jnp.bfloat16)], axis=1
+        ),
+        "shard",
+        scatter_dimension=0,
+        tiled=True,
+    )
+    d_values = d_kv[:, D:].astype(jnp.float32)
+    gqkv_half = jnp.concatenate([d_query.astype(jnp.bfloat16), d_kv], axis=1)
+    d_ln_one = matmul(gqkv_half, full_qkv)
+    grad_input = (d_resid + norm_backward(d_ln_one, normed_one, inv_one, gain_one)).astype(
+        jnp.bfloat16
+    )
+    small_rows = jnp.stack(
+        [
+            jnp.sum(d_ln_one * normed_one, axis=0),
+            jnp.sum(d_ln_one, axis=0),
+            jnp.sum(d_query, axis=0),
+            jnp.sum(d_values, axis=0),
+            jnp.sum(d_resid, axis=0),
+            jnp.sum(d_ln_two * normed_two, axis=0),
+            jnp.sum(d_ln_two, axis=0),
+        ]
+    )
+    small_grad = jnp.concatenate(
+        [small_rows, jnp.sum(d_pre, axis=0).reshape(4, D), jnp.sum(grad_z, axis=0)[None]], axis=0
+    )
+    small_send = jnp.swapaxes(
+        pad_rows(small_grad.astype(jnp.bfloat16).astype(jnp.float32), eight(small_count)).reshape(
+            -1, n_shard, rows_own
+        ),
+        0,
+        1,
+    )
+
+    def weight_grad(left, right):
+        return outer_sum(left, right).astype(jnp.bfloat16).reshape(n_dp, -1, unit, D)
+
+    mixed = jnp.concatenate(
+        [
+            weight_grad(gqkv_half, ln_one_half),
+            weight_grad(gh_half, attended),
+            weight_grad(gu_half, ln_two_half),
+        ],
+        axis=1,
+    ).reshape(n_dp, n_shard, PIECES - 1, unit, D)
+    proj_grads = jnp.stack([weight_grad(gz_half, part) for part in act_parts], axis=1)
+    swapped, proj_sum, small_sum = reduce_rows(
+        jnp.concatenate([mixed, proj_grads], axis=2), small_send, n_dp, n_shard
+    )
+    mixed_sum = swapped.reshape(-1, rows_own).astype(jnp.float32)
+    grad_qkv = mixed_sum[:cols_qkv].T
+    grad_attn_out = mixed_sum[cols_qkv : cols_qkv + cols_out].T
+    grad_fc = mixed_sum[cols_qkv + cols_out :].T
+    grad_proj = proj_sum.astype(jnp.float32).T
+    grad_small = small_sum[:small_count]
+    upd_qkv = adam_update(w_qkv, moment_qkv, second_qkv, grad_qkv, WEIGHT_DECAY)
+    upd_out = adam_update(w_attn_out, moment_attn_out, second_attn_out, grad_attn_out, WEIGHT_DECAY)
+    upd_fc = adam_update(w_fc, moment_fc, second_fc, grad_fc, WEIGHT_DECAY)
+    upd_proj = adam_update(w_proj, moment_proj, second_proj, grad_proj, WEIGHT_DECAY)
+    upd_small = adam_update(small_w, moment_small, second_small, grad_small, 0.0)
+    return (
+        out_act,
+        grad_input,
+        grad_qkv,
+        grad_attn_out,
+        grad_fc,
+        grad_proj,
+        grad_small,
+        upd_qkv[0],
+        upd_out[0],
+        upd_fc[0],
+        upd_proj[0],
+        upd_small[0],
+        upd_qkv[1],
+        upd_out[1],
+        upd_fc[1],
+        upd_proj[1],
+        upd_small[1],
+        upd_qkv[2],
+        upd_out[2],
+        upd_fc[2],
+        upd_proj[2],
+        upd_small[2],
+    )
+
+
 def solution(mesh):
     return jax.shard_map(
         on_device,

time: 778 us -> 560 us (0.72)
  waiting for transfers between devices: 427 us -> 0.82 us
  Pallas kernels: 31.2 us -> 292 us
  blocking collectives: 47.4 us -> 0 us
  local copies, waits for them, and re-layouts: 147 us -> 105 us
  other arithmetic: 30.9 us -> 56.3 us
  matrix products: 67.7 us -> 80.3 us
    pallas_call x2, Pallas kernels: 31.2 us -> 292 us  [the longest x1 174 us: reduce_rows(): pl.pallas_call(lambda *refs: reduce_kernel(n_dp, n_shard, *refs), out_sha...]
    unnamed x6 -> x3, waiting for transfers between devices: 252 us -> 0.03 us
    all_gather x1 -> x0, waiting for transfers between devices: 169 us -> none  [on_device(): lax.all_gather(packed, axes, axis=0, tiled=False)]
    psum x1 -> x0, blocking collectives: 47.4 us -> none  [on_device(): lax.psum(small_grad.astype(jnp.bfloat16).astype(jnp.float32), axes)]
    concatenate x1 -> x2, other arithmetic: 1.01 us -> 38.7 us  [the longest x1 19.7 us: on_device(): jnp.concatenate([weight_grad(gqkv_half, ln_one_half), weight_grad(gh_half...]
    unnamed x254 -> x113, local copies, waits for them, and re-layouts: 59 us -> 22.6 us
    convert_element_type x2, local copies, waits for them, and re-layouts: 0.4 us -> 25.6 us  [weight_grad(): outer_sum(left, right).astype(jnp.bfloat16).reshape(n_dp, -1, unit, D)]
    reshape x27 -> x0, local copies, waits for them, and re-layouts: 24.5 us -> none  [the longest x7 7.58 us: rest_cut(): return jnp.swapaxes(product.reshape(n_dp, count, n_shard, rest), 1, 2)]
  transfers between devices with their start and end apart: 4 -> 2, of which waited for: 4 -> 1; matrix products, arithmetic and copies ran while one was open for 8% -> 12% of each run, Pallas kernels for 0% -> 0%
where the time goes in v1:
time: 560 us; the launch traced here: 550 us
  Pallas kernels  292 us (52%)
  local copies, waits for them, and re-layouts  105 us (19%)
  matrix products  80.3 us (14%)
  other arithmetic  56.3 us (10%)
  between operations  15.3 us (3%)
    pallas_call x1, Pallas kernels, reduce_rows(): pl.pallas_call(lambda *refs: reduce_kernel(n_dp, n_shard, *refs), out_sha...  174 us
    pallas_call x1, Pallas kernels, gather_rows(): pl.pallas_call(lambda *refs: gather_kernel(n_dp, n_shard, *refs), out_sha...  118 us
    convert_element_type x2, local copies, waits for them, and re-layouts, weight_grad(): outer_sum(left, right).astype(jnp.bfloat16).reshape(n_dp, -1, unit, D)  25.6 us
    dot_general x7, matrix products, back_product(): lax.dot_general(left_rows, right_rows, (((1,), (1,)), ((), ())), preferre...  23.2 us
    dot_general x7, matrix products, outer_sum(): lax.dot_general(left_rows, right_rows, (((0,), (0,)), ((), ())), preferre...  23.2 us
    unnamed x113, local copies, waits for them, and re-layouts  22.6 us
    concatenate x1, other arithmetic, on_device(): jnp.concatenate([weight_grad(gqkv_half, ln_one_half), weight_grad(gh_half...  19.7 us
    dot_general x7, matrix products, matmul(): return jnp.dot(left_rows, right_rows, preferred_element_type=jnp.float32)  19.5 us
  transfers between devices with their start and end apart: 2, of which 1 were waited for; matrix products, arithmetic and copies ran while one was open for 12% of the time, Pallas kernels for 0%

profile of v1, /device:TPU:14, one launch (start us, length us, event | category | flops | bytes accessed | tf_op | source)
XLA Modules:
  0.0 549.7 jit_solution(10150409787788277047)
XLA Ops:
  7.3 1.2 convert_reduce_fusion
  8.5 1.1 fusion.47
  11.4 1.1 convert_bitcast_fusion.3
  13.5 117.9 %shard_map.345 = (bf16[8,4,3,136,1088]{4,3,2,1,0:T(8,128)(2,1)S(1)}, bf16[4,16,272]{2,1,0:T(8,128)(2,1)S(1)}) custom-call(bf16[4,2,136,272]{3,2,1,0:T(8,128)(2,1)S(1)} %bitcast.92, bf16[136,1088]{1,0:T(8,128)(2,1)S(1)} %convert_bitcast_fusion.2.refs_1_, bf16[16,272]{1,0:T(8,128)(2,1)S(1)} %pad.9.refs_2_), custom_call_target="tpu_custom_call" | custom-call | tf_op jit(solution)/shard_map/pallas_call | solution.py:786
  131.5 9.9 %copy-done = bf16[8,4,3,136,1088]{4,3,2,1,0:T(8,128)(2,1)} copy-done((bf16[8,4,3,136,1088]{4,3,2,1,0:T(8,128)(2,1)}, bf16[8,4,3,136,1088]{4,3,2,1,0:T(8,128)(2,1)S(1)}, u32[]{:S(2)}) %copy-start) | copy-done | bytes 28409880
  141.9 17.6 %slice.111 = bf16[8,4,2,136,1088]{4,3,2,1,0:T(8,128)(2,1)} slice(bf16[8,4,3,136,1088]{4,3,2,1,0:T(8,128)(2,1)} %copy-done), slice={[0:8], [0:4], [0:2], [0:136], [0:1088]} | slice | bytes 37879808 | tf_op jit(solution)/shard_map/slice | solution.py:1186
  159.5 6.7 %slice.141 = bf16[8,3,136,1088]{3,2,1,0:T(8,128)(2,1)} slice(bf16[8,8,136,1088]{3,2,1,0:T(8,128)(2,1)} %bitcast.94), slice={[0:8], [0:3], [0:136], [0:1088]} | slice | bytes 14204928 | tf_op jit(solution)/shard_map/slice | solution.py:1187
  166.3 5.4 fusion.1
  173.6 1.9 slice.140
  175.5 8.4 %slice.155 = bf16[8,4,136,1088]{3,2,1,0:T(8,128)(2,1)} slice(bf16[8,8,136,1088]{3,2,1,0:T(8,128)(2,1)} %bitcast.96), slice={[0:8], [4:8], [0:136], [0:1088]} | slice | bytes 18939904 | tf_op jit(solution)/shard_map/slice | solution.py:1189
  185.3 5.6 %fusion.99 = (bf16[8,1,1,136,1088]{4,3,2,1,0:T(8,128)(2,1)S(1)}, bf16[8,1,1,136,1088]{4,3,2,1,0:T(8,128)(2,1)S(1)}, bf16[8,1,1,136,1088]{4,3,2,1,0:T(8,128)(2,1)S(1)}, bf16[8,1,1,136,1088]{4,3,2,1,0:T(8,128)(2,1)S(1)}) fusion(bf16[8,4,3,136,1088]{4,3,2,1,0:T(8,128)(2,1)} %copy-done), kind=kLoop, calls=%fused_computation.174 | loop fusion | bytes 18939904 | tf_op jit(solution)/shard_map/slice | solution.py:1190
  191.0 2.0 fusion.77
  192.9 2.1 fusion.75
  195.0 1.4 fusion.79
  196.5 1.4 fusion.81
  197.9 4.2 concatenate.27
  203.1 3.1 fusion.100
  206.3 6.2 %fusion.3 = f32[17,128,512]{2,1,0:T(8,128)} fusion(pred[128,512]{1,0:T(8,128)(4,1)S(1)} %fusion.58, bf16[128,17,64]{0,2,1:T(8,128)(2,1)S(1)} %bitcast.138, bf16[512,17,64]{0,2,1:T(8,128)(2,1)} %bitcast.128), kind=kOutput, calls=%fused_computation.15 | convolution fusion | flops 290785920 | bytes 5914624 | tf_op jit(solution)/shard_map/reduce_sum | solution.py:82
  212.5 3.6 convolution_convert_fusion.10
  217.2 12.8 %fusion.96 = (bf16[4352]{0:T(1024)(128)(2,1)S(1)}, bf16[128,4352]{1,0:T(8,128)(2,1)S(1)}, bf16[128,4352]{1,0:T(8,128)(2,1)}) fusion(f32[128,4352]{1,0:T(8,128)S(1)} %copy-done.30, f32[4352]{0:T(1024)S(1)} %add.215, bf16[4352,1088]{1,0:T(8,128)(2,1)} %bitcast.98, f32[128,1088]{0,1:T(8,128)S(1)} %get-tuple-element.171, f32[1088]{0:T(1024)S(1)} %add.212, ...), kind=kOutput, calls=%fused_computation.172 | convolution fusion | flops 1255739136 | bytes 14519296 | tf_op jit(solution)/shard_map/dot_general | solution.py:32
  230.1 4.3 multiply_reduce_fusion
  235.0 1.1 convolution_convert_fusion.7
  238.9 1.5 pad_maximum_fusion.1
  240.4 4.1 copy.106
  244.8 2.9 fusion.101
  247.8 6.7 %convolution_convert_fusion = bf16[4352,1088]{0,1:T(8,128)(2,1)} fusion(bf16[128,4352]{1,0:T(8,128)(2,1)} %copy-done.21, f32[128,1088]{0,1:T(8,128)S(1)} %get-tuple-element.171, f32[1088]{0:T(1024)S(1)} %add.212, f32[1088]{0:T(1024)S(1)} %mul.337, f32[128]{0:T(128)S(1)} %add_rsqrt_fusion, f32[128]{0:T(128)S(1)} %broadcast_multiply_fusion.4), kind=kOutput, calls=%fused_computation.3 | convolution fusion | flops 1217585152 | bytes 11150848 | tf_op jit(solution)/shard_map/dot_general | solution.py:26
  254.5 14.5 %copy.94 = bf16[4352,1088]{1,0:T(8,128)(2,1)} copy(bf16[4352,1088]{0,1:T(8,128)(2,1)} %convolution_convert_fusion) | data formatting | bytes 18939904 | tf_op jit(solution)/shard_map/convert_element_type | solution.py:1285
  269.0 1.9 convolution_convert_fusion.5
  270.9 2.3 convolution_convert_fusion.4
  273.2 2.3 convolution_convert_fusion.3
  275.5 2.3 convolution_convert_fusion.2
  277.8 2.3 convolution_convert_fusion.6
  285.2 1.6 fusion.10
  286.9 1.4 copy.107
  288.4 7.2 %fusion.46 = (bf16[1088]{0:T(1024)(128)(2,1)S(1)}, f32[128]{0:T(128)S(1)}, f32[128]{0:T(128)S(1)}, bf16[1088]{0:T(1024)(128)(2,1)S(1)}, f32[128,1088]{0,1:T(8,128)}) fusion(bf16[128,1088]{0,1:T(8,128)(2,1)S(1)} %copy-done.16, f32[128]{0:T(128)S(1)} %add_rsqrt_fusion.1, f32[128]{0:T(128)S(1)} %broadcast_multiply_fusion.5, f32[1088]{0:T(1024)S(1)} %mul.329, ...), kind=kOutput, calls=%fused_computation.91 | convolution fusion | flops 912176768 | bytes 8784384 | tf_op jit(solution)/shard_map/dot_general | solution.py:38
  295.6 5.4 convolution_convert_fusion.1
  302.0 11.1 %copy.93 = bf16[3264,1088]{1,0:T(8,128)(2,1)} copy(bf16[3264,1088]{0,1:T(8,128)(2,1)} %convolution_convert_fusion.1) | data formatting | bytes 14204928 | tf_op jit(solution)/shard_map/convert_element_type | solution.py:1285
  313.1 19.7 %pad_maximum_fusion = bf16[8,8,136,1088]{3,2,1,0:T(8,128)(2,1)} fusion(bf16[8,4,136,1088]{3,2,1,0:T(8,128)(2,1)} %bitcast.102, bf16[8,1,136,1088]{3,2,1,0:T(8,128)(2,1)} %bitcast.122, bf16[8,3,136,1088]{3,2,1,0:T(8,128)(2,1)} %bitcast.107), kind=kLoop, calls=%fused_computation.2 | loop fusion | flops 18939904 | bytes 37879808 | tf_op jit(solution)/shard_map/concatenate | solution.py:1287
  332.8 19.0 %maximum_maximum_fusion.refs_0_ = bf16[8,4,3,136,1088]{4,3,2,1,0:T(8,128)(2,1)} fusion(bf16[8,1,1,136,1088]{4,3,2,1,0:T(8,128)(2,1)S(1)} %bitcast.119, bf16[8,1,1,136,1088]{4,3,2,1,0:T(8,128)(2,1)S(1)} %bitcast.118, bf16[8,1,1,136,1088]{4,3,2,1,0:T(8,128)(2,1)S(1)} %bitcast.117, bf16[8,1,1,136,1088]{4,3,2,1,0:T(8,128)(2,1)S(1)} %bitcast.116, ...), kind=kLoop, calls=%fused_computation.1 | loop fusion | flops 56819712 | bytes 56819712 | tf_op jit(solution)/shard_map/concatenate | solution.py:1297
  351.8 173.7 %shard_map.346 = (bf16[4,2,136,272]{3,2,1,0:T(8,128)(2,1)}, bf16[136,1088]{1,0:T(8,128)(2,1)}, f32[16,272]{1,0:T(8,128)}) custom-call(bf16[8,4,3,136,1088]{4,3,2,1,0:T(8,128)(2,1)} %maximum_maximum_fusion.refs_0_, f32[4,16,272]{2,1,0:T(8,128)} %bitcast.142), custom_call_target="tpu_custom_call" | custom-call | tf_op jit(solution)/shard_map/pallas_call | solution.py:1077
  525.5 2.0 slice.164
  527.7 1.5 copy.97
  530.1 2.2 copy.101
  532.2 2.1 multiply_subtract_fusion.3
  534.4 2.0 fusion.45
  537.1 1.5 multiply_subtract_fusion.2
  538.6 1.7 multiply_subtract_fusion
  540.9 1.6 multiply_subtract_fusion.1
  (180 shorter events, 20.9 us)
Async XLA Ops:
  7.2 5.3 copy-start.28
  7.2 5.4 copy-start.25
  7.2 195.9 %all-gather.2.cloned.1.call-start = ((), (), s32[]{:S(2)}) async-start(), calls=%async_computation.1 | async-start | bytes 2785280 | tf_op jit(solution)/shard_map/all_gather | solution.py:1214
  131.5 9.9 %copy-start = (bf16[8,4,3,136,1088]{4,3,2,1,0:T(8,128)(2,1)}, bf16[8,4,3,136,1088]{4,3,2,1,0:T(8,128)(2,1)S(1)}, u32[]{:S(2)}) copy-start(bf16[8,4,3,136,1088]{4,3,2,1,0:T(8,128)(2,1)S(1)} %get-tuple-element.28) | copy-start | bytes 85229568
  159.5 6.8 %copy-start.14 = (bf16[128,1088]{0,1:T(8,128)(2,1)S(1)}, bf16[128,1088]{0,1:T(8,128)(2,1)}, u32[]{:S(2)}) copy-start(bf16[128,1088]{0,1:T(8,128)(2,1)} %param.18) | copy-start | bytes 835588
  173.5 113.3 %reduce-scatter.4.cloned.1.call-start = ((), (), s32[]{:S(2)}) async-start(), calls=%async_computation.2 | async-start | bytes 2785280
  175.5 9.8 %copy-start.49 = (s32[512]{0:T(512)S(1)}, s32[512]{0:T(512)}, u32[]{:S(2)}) copy-start(s32[512]{0:T(512)} %param.20) | copy-start | bytes 6148
  184.9 21.4 %copy-start.33 = (bf16[128,1088]{0,1:T(8,128)(2,1)}, bf16[128,1088]{0,1:T(8,128)(2,1)S(1)}, u32[]{:S(2)}) copy-start(bf16[128,1088]{0,1:T(8,128)(2,1)S(1)} %slice.149) | copy-start | bytes 835588
  185.3 5.6 %copy-start.3 = (bf16[128,1088]{0,1:T(8,128)(2,1)S(1)}, bf16[128,1088]{0,1:T(8,128)(2,1)}, u32[]{:S(2)}) copy-start(bf16[128,1088]{0,1:T(8,128)(2,1)} %param.19) | copy-start | bytes 835588
  190.9 4.1 copy-start.1
  190.9 4.1 copy-start.4
  190.9 4.1 copy-start.6
  190.9 5.5 %copy-start.8 = (bf16[8,1,1,136,1088]{4,3,2,1,0:T(8,128)(2,1)}, bf16[8,1,1,136,1088]{4,3,2,1,0:T(8,128)(2,1)S(1)}, u32[]{:S(2)}) copy-start(bf16[8,1,1,136,1088]{4,3,2,1,0:T(8,128)(2,1)S(1)} %get-tuple-element.163) | copy-start | bytes 7102468
  212.5 3.7 copy-start.15
  212.5 4.7 copy-start.30
  216.1 19.9 %copy-start.22 = (bf16[17,64,128]{2,1,0:T(8,128)(2,1)}, bf16[17,64,128]{2,1,0:T(8,128)(2,1)S(1)}, u32[]{:S(2)}) copy-start(bf16[17,64,128]{2,1,0:T(8,128)(2,1)S(1)} %convolution_convert_fusion.10) | copy-start | bytes 835588
  216.2 13.9 %slice-start = ((s8[10027008]{0:T(1024)(128)(4,1)}), s8[4194304]{0:T(1024)(128)(4,1)S(1)}, s32[]{:S(2)}) async-start(s8[10027008]{0:T(1024)(128)(4,1)} %bitcast.99), calls=%async_computation.3 | async-start | bytes 8388608
  216.2 20.0 %slice-start.3 = ((s8[4456448]{0:T(1024)(128)(4,1)}), s8[4194304]{0:T(1024)(128)(4,1)S(1)}, s32[]{:S(2)}) async-start(s8[4456448]{0:T(1024)(128)(4,1)} %bitcast.103), calls=%async_computation.6 | async-start | bytes 8388608
  217.2 12.9 %slice-start.1 = ((s8[10027008]{0:T(1024)(128)(4,1)}), s8[4194304]{0:T(1024)(128)(4,1)S(1)}, s32[]{:S(2)}) async-start(s8[10027008]{0:T(1024)(128)(4,1)} %bitcast.99), calls=%async_computation.4 | async-start | bytes 8388608
  217.2 12.9 %slice-start.2 = ((s8[10027008]{0:T(1024)(128)(4,1)}), s8[1638400]{0:T(1024)(128)(4,1)S(1)}, s32[]{:S(2)}) async-start(s8[10027008]{0:T(1024)(128)(4,1)} %bitcast.99), calls=%async_computation.5 | async-start | bytes 3276800
  217.2 19.0 %slice-start.4 = ((s8[4456448]{0:T(1024)(128)(4,1)}), s8[262144]{0:T(1024)(128)(4,1)S(1)}, s32[]{:S(2)}) async-start(s8[4456448]{0:T(1024)(128)(4,1)} %bitcast.103), calls=%async_computation.7 | async-start | bytes 524288
  230.1 4.3 copy-start.21
  269.0 1.9 copy-start.20
  275.5 2.3 copy-start.18
  275.5 2.3 copy-start.23
  277.8 2.3 copy-start.9
  285.2 3.1 copy-start.16
  288.4 7.2 %copy-start.35 = (bf16[128,17,64]{0,2,1:T(8,128)(2,1)S(1)}, bf16[128,17,64]{0,2,1:T(8,128)(2,1)}, u32[]{:S(2)}) copy-start(bf16[128,17,64]{0,2,1:T(8,128)(2,1)} %get-tuple-element.168) | copy-start | bytes 835588
  313.1 19.7 %copy-start.10 = (bf16[1088,1088]{1,0:T(8,128)(2,1)S(1)}, bf16[1088,1088]{1,0:T(8,128)(2,1)}, u32[]{:S(2)}) copy-start(bf16[1088,1088]{1,0:T(8,128)(2,1)} %convolution_convert_fusion.4) | copy-start | bytes 7102468
  313.1 19.7 %copy-start.11 = (bf16[1088,1088]{1,0:T(8,128)(2,1)S(1)}, bf16[1088,1088]{1,0:T(8,128)(2,1)}, u32[]{:S(2)}) copy-start(bf16[1088,1088]{1,0:T(8,128)(2,1)} %convolution_convert_fusion.3) | copy-start | bytes 7102468
  313.1 19.7 %copy-start.12 = (bf16[1088,1088]{1,0:T(8,128)(2,1)S(1)}, bf16[1088,1088]{1,0:T(8,128)(2,1)}, u32[]{:S(2)}) copy-start(bf16[1088,1088]{1,0:T(8,128)(2,1)} %convolution_convert_fusion.2) | copy-start | bytes 7102468
  525.5 2.0 copy-start.24
  527.6 4.6 copy-start.36
  529.1 9.4 %copy-start.27 = (f32[544,272]{0,1:T(8,128)}, f32[544,272]{0,1:T(8,128)S(1)}, u32[]{:S(2)}) copy-start(f32[544,272]{0,1:T(8,128)S(1)} %copy.97) | copy-start | bytes 1775620
  529.2 5.2 copy-start.19
  530.0 6.3 %copy-start.45 = (f32[12,272]{1,0:T(8,128)S(1)}, f32[12,272]{1,0:T(8,128)}, u32[]{:S(2)}) copy-start(f32[12,272]{1,0:T(8,128)} %param.25) | copy-start | bytes 39172
  530.0 6.3 %copy-start.46 = (f32[12,272]{1,0:T(8,128)S(1)}, f32[12,272]{1,0:T(8,128)}, u32[]{:S(2)}) copy-start(f32[12,272]{1,0:T(8,128)} %param.30) | copy-start | bytes 39172
  530.1 6.3 %copy-start.47 = (f32[12,272]{1,0:T(8,128)S(1)}, f32[12,272]{1,0:T(8,128)}, u32[]{:S(2)}) copy-start(f32[12,272]{1,0:T(8,128)} %param.35) | copy-start | bytes 39172
  530.1 6.3 %copy-start.48 = (f32[16,272]{1,0:T(8,128)S(1)}, f32[16,272]{1,0:T(8,128)}, u32[]{:S(2)}) copy-start(f32[16,272]{1,0:T(8,128)} %get-tuple-element.31) | copy-start | bytes 52228
  532.2 4.8 copy-start.31
  532.2 4.8 copy-start.32
  532.2 4.8 copy-start.42
  532.2 4.8 copy-start.43
  536.3 2.2 copy-start.26
  536.3 2.2 copy-start.38
  536.3 2.2 copy-start.39
  538.6 2.1 copy-start.41
  538.6 2.3 copy-start.44
  (9 other events, 12.7 us)
Sparse Core Ops, SparseCore 0:
  173.6 29.4 all-gather.1
  244.7 36.9 reduce-scatter.3

commit v2 on v1

--- a/solution.py
+++ b/solution.py
@@ -534,6 +534,7 @@
 MESH_ID = pl.DeviceIdType.MESH
 COLS = 2
 PIECES = 3
+SLOTS = 4
 
 
 def place():
@@ -699,11 +700,12 @@
         copy(4, zs, fa, 0, k).start()
 
     def from_near(zs):
-        pass_on(zs, 1, 0, False, False, False)
+        for k in (1, 0):
+            pass_on(zs, 1, k, False, False, False)
 
     def from_far(zs):
         def step(j, carry):
-            fa, k = j // PIECES, PIECES - 1 - j % PIECES
+            fa, k = j % 2, PIECES - 1 - j // 2
             arrived(zs, fa, 1, k)
             copy(4, zs, fa, 1, k).start()
             return carry
@@ -711,7 +713,6 @@
         lax.fori_loop(0, 2 * PIECES, step, 0)
 
     pass_on(z, 1, 2, True, True, False)
-    pass_on(z, 1, 1, True, True, False)
     from_near(z)
     for delta in range(1, depth):
         for sign in (-1, 1):
@@ -719,8 +720,8 @@
 
             @pl.when((zs >= 0) & (zs < depth))
             def _():
-                for k, fa in ((2, 0), (1, 0), (0, 0), (2, 1), (1, 1)):
-                    pass_on(zs, fa, k, sign < 0, sign > 0, k == 0)
+                for k, fa in ((2, 0), (2, 1), (1, 0), (0, 0)):
+                    pass_on(zs, fa, k, sign < 0, sign > 0, k < 2)
 
         for sign in (-1, 1):
             zs = z + sign * delta
@@ -752,7 +753,7 @@
     def finish(zs, carry):
         for fa in range(2):
             for k in range(PIECES):
-                if k > 0 or fa == 0:
+                if k == 2 or fa == 0:
 
                     @pl.when((z < depth - 1) & (zs <= z))
                     def _():
@@ -763,7 +764,7 @@
                         copy(3, zs, fa, 0, k).wait_send()
 
                 if fa == 0:
-                    if k == 0:
+                    if k < 2:
                         copy(0, zs, fa, 0, k).wait_send()
                     else:
 
@@ -805,7 +806,7 @@
             pltpu.SemaphoreType.DMA((count,)),
         ],
         compiler_params=pltpu.CompilerParams(
-            collective_id=0, has_side_effects=True, vmem_limit_bytes=24 * 1024 * 1024
+            collective_id=0, has_side_effects=True, vmem_limit_bytes=60 * 1024 * 1024
         ),
     )(cut, proj, small)
 
@@ -885,7 +886,7 @@
         return remote(total.at[spot(zq, 1, 0, k)], from_near.at[slot], near_sem, slot, near)
 
     def line_copy(way, zq, fa, k):
-        slot = (way * depth + zq) * 5 + (0 if k == 0 else 2 * k - 1 + fa)
+        slot = (way * depth + zq) * SLOTS + k + fa
         return remote(
             total.at[spot(zq, fa, 0, k)],
             from_line.at[slot],
@@ -961,7 +962,7 @@
                 @pl.when(z < depth - 1)
                 def _():
                     line_copy(1, zq, fa, k).wait_recv()
-                    add(spot(zq, fa, 0, k), from_line.at[(depth + zq) * 5 + slot_of(fa, k)])
+                    add(spot(zq, fa, 0, k), from_line.at[(depth + zq) * SLOTS + k + fa])
 
                 line_copy(1, zq, fa, k).start()
 
@@ -970,55 +971,48 @@
                 @pl.when(z > 0)
                 def _():
                     line_copy(0, zq, fa, k).wait_recv()
-                    add(spot(zq, fa, 0, k), from_line.at[zq * 5 + slot_of(fa, k)])
+                    add(spot(zq, fa, 0, k), from_line.at[zq * SLOTS + k + fa])
 
                 line_copy(0, zq, fa, k).start()
-
-        def slot_of(fa, k):
-            return 0 if k == 0 else 2 * k - 1 + fa
 
         def take_far(fa, k):
             far_copy(zq, fa, k).wait_recv()
             add(spot(zq, fa, 0, k), from_far.at[(zq * 2 + fa) * PIECES + k])
 
-        take_far(1, 0)
-        near_copy(zq, 0, zq).start()
-        take_far(0, 0)
-        for k in (1, 2):
-            for fa in (1, 0):
-                take_far(fa, k)
-                line_step(fa, k)
-        near_copy(zq, 0, zq).wait_recv()
-        add(spot(zq, 0, 0, 0), from_near.at[zq])
-        line_step(0, 0)
+        for k in (0, 1):
+            take_far(1, k)
+            near_copy(zq, k, k * depth + zq).start()
+            take_far(0, k)
+        for fa in (1, 0):
+            take_far(fa, 2)
+            line_step(fa, 2)
+        for k in (0, 1):
+            near_copy(zq, k, k * depth + zq).wait_recv()
+            add(spot(zq, 0, 0, k), from_near.at[k * depth + zq])
+            line_step(0, k)
         return carry
 
     lax.fori_loop(0, depth, level_step, 0)
 
     def last(fa, k):
-        number = 0 if k == 0 else 2 * k - 1 + fa
+        number = k + fa
 
         @pl.when(z < depth - 1)
         def _():
             line_copy(1, z, fa, k).wait_recv()
-            add(spot(z, fa, 0, k), from_line.at[(depth + z) * 5 + number])
+            add(spot(z, fa, 0, k), from_line.at[(depth + z) * SLOTS + number])
 
         @pl.when(z > 0)
         def _():
             line_copy(0, z, fa, k).wait_recv()
-            add(spot(z, fa, 0, k), from_line.at[z * 5 + number])
-
-    for k in (1, 2):
-        last(1, k)
-        near_copy(z, k, depth + k - 1).start()
-    for k in (1, 0, 2):
+            add(spot(z, fa, 0, k), from_line.at[z * SLOTS + number])
+
+    last(1, 2)
+    near_copy(z, 2, 2 * depth).start()
+    for k in (0, 1):
         last(0, k)
-        if k > 0:
-            near_copy(z, k, depth + k - 1).wait_recv()
-            add(spot(z, 0, 0, k), from_near.at[depth + k - 1])
-        if k < 2:
-            for part in range(n_shard):
-                cut[part, k] = total[spot(z, 0, 0, k), :, part * lanes : (part + 1) * lanes]
+        for part in range(n_shard):
+            cut[part, k] = total[spot(z, 0, 0, k), :, part * lanes : (part + 1) * lanes]
 
     def swap_copy(step):
         peer = (s + step) % n_shard
@@ -1028,6 +1022,9 @@
         swap_copy(step).start()
     own_cut = pltpu.make_async_copy(cut.at[s], swap_out.at[s], own_sem.at[2])
     own_cut.start()
+    last(0, 2)
+    near_copy(z, 2, 2 * depth).wait_recv()
+    add(spot(z, 0, 0, 2), from_near.at[2 * depth])
     proj_out[...] = total[spot(z, 0, 0, 2)]
     own_all.wait()
     for step in range(1, n_dp):
@@ -1043,7 +1040,7 @@
                 for fb in range(2):
                     sib_copy(zq, fa, fb, k).wait_send()
                 far_copy(zq, fa, k).wait_send()
-                if k > 0 or fa == 0:
+                if k == 2 or fa == 0:
 
                     @pl.when(zq < z)
                     def _():
@@ -1053,12 +1050,12 @@
                     def _():
                         line_copy(0, zq, fa, k).wait_send()
 
-        near_copy(zq, 0, zq).wait_send()
+        for k in (0, 1):
+            near_copy(zq, k, k * depth + zq).wait_send()
         return carry
 
     lax.fori_loop(0, depth, finish, 0)
-    for k in (1, 2):
-        near_copy(z, k, depth + k - 1).wait_send()
+    near_copy(z, 2, 2 * depth).wait_send()
 
 
 def reduce_rows(grads, small, n_dp, n_shard):
@@ -1090,8 +1087,8 @@
             pieces(count),
             pieces(count),
             pieces(depth * 2 * PIECES),
-            pieces(depth + 2),
-            pieces(2 * depth * 5),
+            pieces(2 * depth + 1),
+            pieces(2 * depth * SLOTS),
             pltpu.VMEM((n_shard, PIECES - 1, piece_rows, lanes), kind),
             pltpu.VMEM(small.shape, small.dtype),
             pltpu.VMEM(small.shape[1:], small.dtype),
@@ -1099,8 +1096,8 @@
             sems(count),
             sems(2, count),
             sems(2, depth * 2 * PIECES),
-            sems(2, depth + 2),
-            sems(2, 2 * depth * 5),
+            sems(2, 2 * depth + 1),
+            sems(2, 2 * depth * SLOTS),
             sems(2, n_shard),
             sems(2, n_shard),
             sems(2, n_dp),
@@ -1110,6 +1107,186 @@
             collective_id=1, has_side_effects=True, vmem_limit_bytes=62 * 1024 * 1024
         ),
     )(grads, small)
+
+
+def block_specs(blocks, unit, width):
+    specs = []
+    for t_start, t_count, k_start, k_count in blocks:
+        specs.append(
+            pl.BlockSpec(
+                (1, t_count, k_count, unit, width),
+                lambda d, t=t_start // t_count, k=k_start // k_count: (d, t, k, 0, 0),
+            )
+        )
+    return specs
+
+
+def block_units(refs, blocks):
+    return [
+        ref[0, t, k]
+        for ref, (t_start, t_count, k_start, k_count) in zip(refs, blocks)
+        for t in range(t_count)
+        for k in range(k_count)
+    ]
+
+
+def block_cost(count, full, rows):
+    elements = count * full.shape[0] * full.shape[3] * full.shape[4]
+    return pl.CostEstimate(
+        flops=2 * elements * rows, bytes_accessed=2 * elements, transcendentals=0
+    )
+
+
+QKV_BLOCKS = ((0, 1, 0, 2), (1, 1, 0, 1))
+OUT_BLOCKS = ((1, 1, 1, 1),)
+FC_BLOCKS = ((2, 2, 0, 2),)
+PROJ_BLOCKS = ((0, 4, 2, 1),)
+
+
+def forward_product(rows_in, full, blocks):
+    n_dp, unit, width = full.shape[0], full.shape[3], full.shape[4]
+    summed = rows_in.ndim == 3
+    count = sum(b[1] * b[3] for b in blocks)
+    rows = rows_in.shape[-2]
+    out_count = 1 if summed else count
+
+    def kernel(rows_ref, *refs):
+        out_ref = refs[-1]
+        total = None
+        for i, block in enumerate(block_units(refs[:-1], blocks)):
+            left = rows_ref[i] if summed else rows_ref[...]
+            product = back_product(block, left)
+            if summed:
+                total = product if total is None else total + product
+            else:
+                out_ref[0, i] = product
+        if summed:
+            out_ref[0, 0] = total
+
+    out = pl.pallas_call(
+        kernel,
+        grid=(n_dp,),
+        in_specs=[pl.BlockSpec(rows_in.shape, lambda d: (0,) * rows_in.ndim)]
+        + block_specs(blocks, unit, width),
+        out_specs=pl.BlockSpec((1, out_count, unit, rows), lambda d: (d, 0, 0, 0)),
+        out_shape=jax.ShapeDtypeStruct((n_dp, out_count, unit, rows), jnp.float32),
+        compiler_params=pltpu.CompilerParams(vmem_limit_bytes=32 * 1024 * 1024),
+        cost_estimate=block_cost(count, full, rows),
+    )(rows_in, *[full] * len(blocks))
+    return out.reshape(n_dp * out_count * unit, rows).T
+
+
+def backward_product(left, full, blocks):
+    n_dp, unit, width = full.shape[0], full.shape[3], full.shape[4]
+    count = sum(b[1] * b[3] for b in blocks)
+    rows = left.shape[-1]
+    summed = left.shape[1] == count
+    out_count = 1 if summed else count
+
+    def kernel(left_ref, *refs):
+        out_ref = refs[-1]
+        products = []
+        for i, block in enumerate(block_units(refs[:-1], blocks)):
+            products.append(outer_sum(left_ref[0, i if summed else 0], block))
+        if summed:
+            products = [sum(products[1:], products[0])]
+        first = pl.program_id(0) == 0
+
+        @pl.when(first)
+        def _():
+            for i, product in enumerate(products):
+                out_ref[i] = product
+
+        @pl.when(jnp.logical_not(first))
+        def _():
+            for i, product in enumerate(products):
+                out_ref[i] += product
+
+    out = pl.pallas_call(
+        kernel,
+        grid=(n_dp,),
+        in_specs=[pl.BlockSpec((1,) + left.shape[1:], lambda d: (d, 0, 0, 0))]
+        + block_specs(blocks, unit, width),
+        out_specs=pl.BlockSpec((out_count, rows, width), lambda d: (0, 0, 0)),
+        out_shape=jax.ShapeDtypeStruct((out_count, rows, width), jnp.float32),
+        compiler_params=pltpu.CompilerParams(vmem_limit_bytes=40 * 1024 * 1024),
+        cost_estimate=block_cost(count, full, rows),
+    )(left, *[full] * len(blocks))
+    return out[0] if summed else out
+
+
+def per_dp(array):
+    return pl.BlockSpec((1,) + array.shape[1:], lambda d: (d,) + (0,) * (array.ndim - 1))
+
+
+def whole(array):
+    return pl.BlockSpec(array.shape, lambda d: (0,) * array.ndim)
+
+
+def late_grads(fc_units, proj_units, fc_rows, act_parts, n_shard):
+    n_dp, _, unit, rows = proj_units.shape
+    width = fc_rows.shape[-1]
+
+    def kernel(fc_ref, proj_ref, rows_ref, act_ref, out_ref):
+        for i in range(4):
+            out_ref[0, 2 + i // 2, i % 2] = matmul(fc_ref[0, i], rows_ref[...]).astype(
+                out_ref.dtype
+            )
+        for t in range(n_shard):
+            out_ref[0, t, PIECES - 1] = matmul(proj_ref[0, 0], act_ref[t]).astype(out_ref.dtype)
+
+    shape = (n_dp, n_shard, PIECES, unit, width)
+    return pl.pallas_call(
+        kernel,
+        grid=(n_dp,),
+        in_specs=[per_dp(fc_units), per_dp(proj_units), whole(fc_rows), whole(act_parts)],
+        out_specs=pl.BlockSpec((1,) + shape[1:], lambda d: (d, 0, 0, 0, 0)),
+        out_shape=jax.ShapeDtypeStruct(shape, jnp.bfloat16),
+        compiler_params=pltpu.CompilerParams(vmem_limit_bytes=40 * 1024 * 1024),
+        cost_estimate=pl.CostEstimate(
+            flops=2 * 8 * n_dp * unit * width * rows,
+            bytes_accessed=2 * math.prod(shape),
+            transcendentals=0,
+        ),
+    )(fc_units, proj_units, fc_rows, act_parts)
+
+
+def early_grads(partial, qkv_units, out_units, qkv_rows, out_rows):
+    n_dp, n_shard, _, unit, width = partial.shape
+    lefts = jnp.concatenate([qkv_units, out_units], axis=1)
+    rights = jnp.stack([qkv_rows, out_rows])
+    rows = qkv_rows.shape[0]
+
+    def kernel(partial_ref, left_ref, right_ref, out_ref):
+        last = pl.program_id(1) == 1
+        out_ref[0, 0, 0] = matmul(left_ref[0, 0], right_ref[0]).astype(out_ref.dtype)
+
+        @pl.when(last)
+        def _():
+            out_ref[0, 0, 1] = matmul(left_ref[0, 1], right_ref[1]).astype(out_ref.dtype)
+
+        @pl.when(jnp.logical_not(last))
+        def _():
+            out_ref[0, 0, 1] = matmul(left_ref[0, 1], right_ref[0]).astype(out_ref.dtype)
+
+    return pl.pallas_call(
+        kernel,
+        grid=(n_dp, 2),
+        in_specs=[
+            pl.BlockSpec(memory_space=pl.ANY),
+            pl.BlockSpec((1, 2, unit, rows), lambda d, j: (d, j, 0, 0)),
+            pl.BlockSpec(rights.shape, lambda d, j: (0, 0, 0)),
+        ],
+        out_specs=pl.BlockSpec((1, 1, 2, unit, width), lambda d, j: (d, j, 0, 0, 0)),
+        out_shape=jax.ShapeDtypeStruct(partial.shape, partial.dtype),
+        input_output_aliases={0: 0},
+        compiler_params=pltpu.CompilerParams(vmem_limit_bytes=40 * 1024 * 1024),
+        cost_estimate=pl.CostEstimate(
+            flops=2 * 4 * n_dp * unit * width * rows,
+            bytes_accessed=2 * 4 * n_dp * unit * width,
+            transcendentals=0,
+        ),
+    )(partial, lefts, rights)
 
 
 def fits(w_qkv, w_attn_out, w_fc, w_proj, n_dp, n_shard):
@@ -1183,11 +1360,10 @@
         n_dp,
         n_shard,
     )
-    units = gathered[:, :, : PIECES - 1].reshape(n_dp, n_shard * 2, unit, D)
-    full_qkv = units[:, :3].reshape(3 * D, D)
-    full_out = units[:, 3].reshape(D, D)
-    full_fc = units[:, 4:].reshape(FF, D)
-    full_proj = [gathered[:, t, PIECES - 1].reshape(D, D) for t in range(n_shard)]
+
+    def by_unit(rows_in):
+        return rows_in.T.reshape(n_dp, -1, unit, rows_in.shape[0])
+
     small_vals = jnp.swapaxes(small_all, 0, 1).reshape(-1, D)[:small_count].astype(jnp.float32)
     gain_one = small_vals[0]
     shift_one = small_vals[1]
@@ -1206,7 +1382,7 @@
     x_rows = tokens_in.astype(jnp.float32)
     normed_one, inv_one, ln_one = norm_forward(x_rows, gain_one, shift_one)
     ln_one_half = ln_one.astype(jnp.bfloat16)
-    qkv_rows = back_product(ln_one_half, full_qkv) + jnp.concatenate(
+    qkv_rows = forward_product(ln_one_half, gathered, QKV_BLOCKS) + jnp.concatenate(
         [q_bias, jnp.zeros_like(q_bias), v_bias]
     )
     queries = qkv_rows[:, :D].astype(jnp.bfloat16)
@@ -1221,27 +1397,28 @@
         & ((own_seg >= 0)[:, None] | (key_pos[None, :] == query_pos[:, None]))
     )
     attended, log_total = attend_forward(queries, key_all, value_all, allowed)
-    resid = x_rows + back_product(attended, full_out) + out_bias
+    resid = x_rows + forward_product(attended, gathered, OUT_BLOCKS) + out_bias
     normed_two, inv_two, ln_two = norm_forward(resid, gain_two, shift_two)
     ln_two_half = ln_two.astype(jnp.bfloat16)
-    pre_act = back_product(ln_two_half, full_fc) + fc_bias
+    pre_act = forward_product(ln_two_half, gathered, FC_BLOCKS) + fc_bias
     act_half = jax.nn.gelu(pre_act, approximate=False).astype(jnp.bfloat16)
-    act_parts = [act_half[:, t * D : (t + 1) * D] for t in range(n_shard)]
-    out_sum = resid + proj_bias
-    for act_part, proj_part in zip(act_parts, full_proj):
-        out_sum = out_sum + back_product(act_part, proj_part)
-    out_act = out_sum.astype(jnp.bfloat16)
+    act_parts = jnp.stack([act_half[:, t * D : (t + 1) * D] for t in range(n_shard)])
+    out_act = (resid + forward_product(act_parts, gathered, PROJ_BLOCKS) + proj_bias).astype(
+        jnp.bfloat16
+    )
     valid = (own_seg >= 0).astype(jnp.float32)
     grad_z = cotangent.astype(jnp.float32) * valid[:, None]
     gz_half = grad_z.astype(jnp.bfloat16)
-    d_pre = jnp.concatenate([matmul(gz_half, part) for part in full_proj], axis=1) * gelu_slope(
-        pre_act
-    )
+    gz_units = by_unit(gz_half)
+    d_act = backward_product(gz_units, gathered, PROJ_BLOCKS)
+    d_pre = jnp.concatenate(list(d_act), axis=1) * gelu_slope(pre_act)
     gu_half = d_pre.astype(jnp.bfloat16)
-    d_ln_two = matmul(gu_half, full_fc)
+    gu_units = by_unit(gu_half)
+    d_ln_two = backward_product(gu_units, gathered, FC_BLOCKS)
     d_resid = grad_z + norm_backward(d_ln_two, normed_two, inv_two, gain_two)
     gh_half = d_resid.astype(jnp.bfloat16)
-    grad_attn = matmul(gh_half, full_out).astype(jnp.bfloat16)
+    gh_units = by_unit(gh_half)
+    grad_attn = backward_product(gh_units, gathered, OUT_BLOCKS).astype(jnp.bfloat16)
     d_query, d_keys_all, d_values_all = attend_backward(
         queries, key_all, value_all, allowed, log_total, attended, grad_attn
     )
@@ -1255,7 +1432,8 @@
     )
     d_values = d_kv[:, D:].astype(jnp.float32)
     gqkv_half = jnp.concatenate([d_query.astype(jnp.bfloat16), d_kv], axis=1)
-    d_ln_one = matmul(gqkv_half, full_qkv)
+    gqkv_units = by_unit(gqkv_half)
+    d_ln_one = backward_product(gqkv_units, gathered, QKV_BLOCKS)
     grad_input = (d_resid + norm_backward(d_ln_one, normed_one, inv_one, gain_one)).astype(
         jnp.bfloat16
     )
@@ -1281,21 +1459,9 @@
         1,
     )
 
-    def weight_grad(left, right):
-        return outer_sum(left, right).astype(jnp.bfloat16).reshape(n_dp, -1, unit, D)
-
-    mixed = jnp.concatenate(
-        [
-            weight_grad(gqkv_half, ln_one_half),
-            weight_grad(gh_half, attended),
-            weight_grad(gu_half, ln_two_half),
-        ],
-        axis=1,
-    ).reshape(n_dp, n_shard, PIECES - 1, unit, D)
-    proj_grads = jnp.stack([weight_grad(gz_half, part) for part in act_parts], axis=1)
-    swapped, proj_sum, small_sum = reduce_rows(
-        jnp.concatenate([mixed, proj_grads], axis=2), small_send, n_dp, n_shard
-    )
+    late = late_grads(gu_units, gz_units, ln_two_half, act_parts, n_shard)
+    grads = early_grads(late, gqkv_units, gh_units, ln_one_half, attended)
+    swapped, proj_sum, small_sum = reduce_rows(grads, small_send, n_dp, n_shard)
     mixed_sum = swapped.reshape(-1, rows_own).astype(jnp.float32)
     grad_qkv = mixed_sum[:cols_qkv].T
     grad_attn_out = mixed_sum[cols_qkv : cols_qkv + cols_out].T

time: 560 us -> 509 us (0.909)
  Pallas kernels: 292 us -> 369 us
  local copies, waits for them, and re-layouts: 105 us -> 40.9 us
  matrix products: 80.3 us -> 20.8 us
  other arithmetic: 56.3 us -> 34.9 us
  waiting for transfers between devices: 0.82 us -> 18.4 us
    pallas_call x0 -> x10, Pallas kernels: none -> 83.5 us  [the longest x4 31.3 us: backward_product(): pl.pallas_call(kernel, grid=(n_dp,), in_specs=[pl.BlockSpec((1,) + left.s...]
    dot_general x21 -> x0, matrix products: 65.9 us -> none  [the longest x7 23.2 us: back_product(): lax.dot_general(left_rows, right_rows, (((1,), (1,)), ((), ())), preferre...]
    slice x6 -> x1, local copies, waits for them, and re-layouts: 40.4 us -> 0.66 us  [on_device(): proj_bias = small_vals[11]]
    concatenate x2, other arithmetic: 38.7 us -> 0.16 us  [the longest x1 0.1 us: early_grads(): lefts = jnp.concatenate([qkv_units, out_units], axis=1)]
    convert_element_type x2 -> x3, local copies, waits for them, and re-layouts: 25.6 us -> 3.87 us  [the longest x2 2.05 us: attend_forward(): attended.reshape(queries.shape[0], H * HD).astype(jnp.bfloat16)]
    pallas_call x1, Pallas kernels: 174 us -> 155 us  [reduce_rows(): pl.pallas_call(lambda *refs: reduce_kernel(n_dp, n_shard, *refs), out_sha...]
    pallas_call x1, Pallas kernels: 118 us -> 130 us  [gather_rows(): pl.pallas_call(lambda *refs: gather_kernel(n_dp, n_shard, *refs), out_sha...]
    unnamed x3, waiting for transfers between devices: 0.03 us -> 9.75 us
  transfers between devices with their start and end apart: 2 -> 2, of which waited for: 1 -> 2; matrix products, arithmetic and copies ran while one was open for 12% -> 3% of each run, Pallas kernels for 0% -> 4%
where the time goes in v2:
time: 509 us; the launch traced here: 499 us
  Pallas kernels  369 us (72%)
  local copies, waits for them, and re-layouts  40.9 us (8%)
  other arithmetic  34.9 us (7%)
  matrix products  20.8 us (4%)
  waiting for transfers between devices  18.4 us (4%)
  between operations  14.8 us (3%)
    pallas_call x1, Pallas kernels, reduce_rows(): pl.pallas_call(lambda *refs: reduce_kernel(n_dp, n_shard, *refs), out_sha...  155 us
    pallas_call x1, Pallas kernels, gather_rows(): pl.pallas_call(lambda *refs: gather_kernel(n_dp, n_shard, *refs), out_sha...  130 us
    pallas_call x4, Pallas kernels, backward_product(): pl.pallas_call(kernel, grid=(n_dp,), in_specs=[pl.BlockSpec((1,) + left.s...  31.3 us
    pallas_call x4, Pallas kernels, forward_product(): pl.pallas_call(kernel, grid=(n_dp,), in_specs=[pl.BlockSpec(rows_in.shape...  28.9 us
    unnamed x95, local copies, waits for them, and re-layouts  15 us
    pallas_call x1, Pallas kernels, late_grads(): pl.pallas_call(kernel, grid=(n_dp,), in_specs=[per_dp(fc_units), per_dp(p...  12.2 us
    pallas_call x1, Pallas kernels, early_grads(): pl.pallas_call(kernel, grid=(n_dp, 2), in_specs=[pl.BlockSpec(memory_spac...  11.1 us
  transfers between devices with their start and end apart: 2, of which 2 were waited for; matrix products, arithmetic and copies ran while one was open for 3% of the time, Pallas kernels for 4%

profile of v2, /device:TPU:14, one launch (start us, length us, event | category | flops | bytes accessed | tf_op | source)
XLA Modules:
  0.0 499.1 jit_solution(4670884978806639152)
XLA Ops:
  9.2 1.1 convert_bitcast_fusion.5
  10.3 1.2 copy.118
  13.1 1.2 copy.120
  14.9 130.2 %shard_map.345 = (bf16[8,4,3,136,1088]{4,3,2,1,0:T(8,128)(2,1)}, bf16[4,16,272]{2,1,0:T(8,128)(2,1)}) custom-call(bf16[4,2,136,272]{3,2,1,0:T(8,128)(2,1)} %bitcast.209, bf16[136,1088]{1,0:T(8,128)(2,1)} %convert_bitcast_fusion.3.refs_1_, bf16[16,272]{1,0:T(8,128)(2,1)} %pad.9.refs_2_), custom_call_target="tpu_custom_call" | custom-call | tf_op jit(solution)/shard_map/pallas_call | solution.py:787
  147.2 7.1 %shard_map.346 = f32[8,3,136,128]{3,2,1,0:T(8,128)S(1)} custom-call(bf16[128,1088]{1,0:T(8,128)(2,1)S(1)} %fusion.45.rows_ref, bf16[8,4,3,136,1088]{4,3,2,1,0:T(8,128)(2,1)} %get-tuple-element.28.refs_0_.refs_1_, bf16[8,4,3,136,1088]{4,3,2,1,0:T(8,128)(2,1)} %get-tuple-element.28.refs_0_.refs_1_), custom_call_target="tpu_custom_call" | custom-call | flops 909115392 | bytes 7102464 | tf_op jit(solution)/shard_map/pallas_call | solution.py:1166
  158.6 9.4 %shard_map.350 = f32[4,128,1088]{2,1,0:T(8,128)S(1)} custom-call(bf16[8,1,136,128]{3,2,1,0:T(8,128)(2,1)S(1)} %bitcast.188, bf16[8,4,3,136,1088]{4,3,2,1,0:T(8,128)(2,1)} %get-tuple-element.28.refs_0_.refs_1_), custom_call_target="tpu_custom_call" | custom-call | flops 1212153856 | bytes 9469952 | tf_op jit(solution)/shard_map/pallas_call | solution.py:1205
  168.2 2.4 concatenate.24
  170.8 8.6 %all-gather.2.cloned.1.call-done = bf16[512,2176]{0,1:T(8,128)(2,1)} async-done(((bf16[128,2176]{0,1:T(8,128)(2,1)}), bf16[512,2176]{0,1:T(8,128)(2,1)}) %all-gather.2.cloned.1.call-update) | async-done | bytes 2228240 | tf_op jit(solution)/shard_map/all_gather | solution.py:1390
  179.4 1.7 fusion.83
  181.2 4.5 fusion.2
  185.6 3.2 convolution_convert_fusion.2
  189.0 5.3 %shard_map.347 = f32[8,1,136,128]{3,2,1,0:T(8,128)S(1)} custom-call(bf16[128,1088]{1,0:T(8,128)(2,1)S(1)} %copy.121.rows_ref, bf16[8,4,3,136,1088]{4,3,2,1,0:T(8,128)(2,1)} %get-tuple-element.28.refs_0_.refs_1_), custom_call_target="tpu_custom_call" | custom-call | flops 303038464 | bytes 2367488 | tf_op jit(solution)/shard_map/pallas_call | solution.py:1166
  195.7 8.2 %shard_map.348 = f32[8,4,136,128]{3,2,1,0:T(8,128)S(1)} custom-call(bf16[128,1088]{1,0:T(8,128)(2,1)S(1)} %add_convert_fusion.rows_ref, bf16[8,4,3,136,1088]{4,3,2,1,0:T(8,128)(2,1)} %get-tuple-element.28.refs_0_.refs_1_), custom_call_target="tpu_custom_call" | custom-call | flops 1212153856 | bytes 9469952 | tf_op jit(solution)/shard_map/pallas_call | solution.py:1166
  204.0 2.0 copy.124
  205.9 8.0 %fusion.78 = (bf16[4352]{0:T(1024)(128)(2,1)S(1)}, bf16[128,4352]{1,0:T(8,128)(2,1)}, bf16[128,4352]{1,0:T(8,128)(2,1)S(1)}) fusion(f32[128,4352]{1,0:T(8,128)} %concatenate.24, f32[4352,128]{0,1:T(8,128)} %copy.124, f32[4352]{0:T(1024)S(1)} %add.210), kind=kLoop, calls=%fused_computation.164 | loop fusion | flops 42888960 | bytes 6710784 | tf_op jit(solution)/shard_map/reduce_sum | solution.py:1452
  213.9 1.7 copy.129
  215.6 8.6 %shard_map.351 = f32[1,128,1088]{2,1,0:T(8,128)S(1)} custom-call(bf16[8,4,136,128]{3,2,1,0:T(8,128)(2,1)S(1)} %bitcast.181, bf16[8,4,3,136,1088]{4,3,2,1,0:T(8,128)(2,1)} %get-tuple-element.28.refs_0_.refs_1_), custom_call_target="tpu_custom_call" | custom-call | flops 1212153856 | bytes 9469952 | tf_op jit(solution)/shard_map/pallas_call | solution.py:1205
  225.0 8.2 %shard_map.349 = f32[8,1,136,128]{3,2,1,0:T(8,128)S(1)} custom-call(bf16[4,128,1088]{2,1,0:T(8,128)(2,1)S(1)} %pad_maximum_fusion.1.rows_ref.act_ref, bf16[8,4,3,136,1088]{4,3,2,1,0:T(8,128)(2,1)} %get-tuple-element.28.refs_0_.refs_1_), custom_call_target="tpu_custom_call" | custom-call | flops 1212153856 | bytes 9469952 | tf_op jit(solution)/shard_map/pallas_call | solution.py:1166
  234.0 2.1 copy.125
  236.1 2.3 fusion.80
  240.0 1.1 copy.130
  241.1 5.9 %shard_map.352 = f32[1,128,1088]{2,1,0:T(8,128)S(1)} custom-call(bf16[8,1,136,128]{3,2,1,0:T(8,128)(2,1)S(1)} %bitcast.186, bf16[8,4,3,136,1088]{4,3,2,1,0:T(8,128)(2,1)} %get-tuple-element.28.refs_0_.refs_1_), custom_call_target="tpu_custom_call" | custom-call | flops 303038464 | bytes 2367488 | tf_op jit(solution)/shard_map/pallas_call | solution.py:1205
  247.8 1.8 copy.132
  249.6 1.1 multiply_reduce_fusion.2
  250.8 2.9 convolution_convert_fusion
  253.7 4.5 multiply_convert_fusion
  258.2 2.1 convolution_convert_fusion.1
  260.3 1.5 pad_maximum_fusion
  261.8 4.1 copy.144
  266.6 1.9 fusion.97
  268.6 1.8 copy.135
  270.6 1.8 copy.141
  272.4 3.6 fusion.84
  276.1 12.2 %shard_map.354.partial_ref = bf16[8,4,3,136,1088]{4,3,2,1,0:T(8,128)(2,1)} custom-call(bf16[8,4,136,128]{3,2,1,0:T(8,128)(2,1)S(1)} %bitcast.182, bf16[8,1,136,128]{3,2,1,0:T(8,128)(2,1)S(1)} %bitcast.189, bf16[128,1088]{1,0:T(8,128)(2,1)S(1)} %add_convert_fusion.rows_ref, bf16[4,128,1088]{2,1,0:T(8,128)(2,1)S(1)} %pad_maximum_fusion.1.rows_ref.act_ref), custom_call_target="tpu_custom_call" | custom-call | flops 2424307712 | bytes 28409856 | tf_op jit(solution)/shard_map/pallas_call | solution.py:1239
  288.5 9.7 %reduce-scatter.4.cloned.1.call-done = bf16[128,2176]{1,0:T(8,128)(2,1)} async-done(((bf16[512,2176]{1,0:T(8,128)(2,1)}), bf16[128,2176]{1,0:T(8,128)(2,1)}) %reduce-scatter.4.cloned.1.call-update) | async-done | bytes 557072
  298.2 1.4 copy.145
  299.8 7.4 %shard_map.353 = f32[1,128,1088]{2,1,0:T(8,128)S(1)} custom-call(bf16[8,3,136,128]{3,2,1,0:T(8,128)(2,1)S(1)} %bitcast.184, bf16[8,4,3,136,1088]{4,3,2,1,0:T(8,128)(2,1)} %get-tuple-element.28.refs_0_.refs_1_, bf16[8,4,3,136,1088]{4,3,2,1,0:T(8,128)(2,1)} %get-tuple-element.28.refs_0_.refs_1_), custom_call_target="tpu_custom_call" | custom-call | flops 909115392 | bytes 7102464 | tf_op jit(solution)/shard_map/pallas_call | solution.py:1205
  309.5 11.1 %shard_map.355.refs_0_ = bf16[8,4,3,136,1088]{4,3,2,1,0:T(8,128)(2,1)} custom-call(bf16[8,4,3,136,1088]{4,3,2,1,0:T(8,128)(2,1)} %shard_map.354.partial_ref, bf16[8,4,136,128]{3,2,1,0:T(8,128)(2,1)S(1)} %pad_maximum_fusion.2.left_ref, bf16[2,128,1088]{2,1,0:T(8,128)(2,1)S(1)} %pad_maximum_fusion.4.right_ref), custom_call_target="tpu_custom_call", output_to_operand_aliasing={{}: (0, {})} | custom-call | flops 1212153856 | bytes 9469952 | tf_op jit(solution)/shard_map/pallas_call | solution.py:1272
  320.6 155.3 %shard_map.356 = (bf16[4,2,136,272]{3,2,1,0:T(8,128)(2,1)}, bf16[136,1088]{1,0:T(8,128)(2,1)}, f32[16,272]{1,0:T(8,128)}) custom-call(bf16[8,4,3,136,1088]{4,3,2,1,0:T(8,128)(2,1)} %shard_map.355.refs_0_, f32[4,16,272]{2,1,0:T(8,128)} %bitcast.214), custom_call_target="tpu_custom_call" | custom-call | tf_op jit(solution)/shard_map/pallas_call | solution.py:1074
  475.9 2.1 slice.129
  478.0 1.3 convert_element_type.160
  480.5 1.4 copy.137
  482.0 1.0 copy.143
  483.0 2.2 multiply_subtract_fusion.3
  485.2 1.6 multiply_subtract_fusion.4
  486.8 1.5 multiply_subtract_fusion.2
  488.4 1.7 multiply_subtract_fusion
  490.6 1.6 multiply_subtract_fusion.1
  (168 shorter events, 21.5 us)
Async XLA Ops:
  7.2 4.6 copy-start.19
  7.2 5.4 %copy-start.16 = (f32[272,544]{1,0:T(8,128)S(1)}, f32[272,544]{1,0:T(8,128)}, u32[]{:S(2)}) copy-start(f32[272,544]{1,0:T(8,128)} %param.23) | copy-start | bytes 1775620
  7.2 172.2 %all-gather.2.cloned.1.call-start = ((), (), s32[]{:S(2)}) async-start(), calls=%async_computation.1 | async-start | bytes 2785280 | tf_op jit(solution)/shard_map/all_gather | solution.py:1390
  11.4 183.1 %copy-start.3 = (bf16[128,1088]{1,0:T(8,128)(2,1)}, bf16[128,1088]{1,0:T(8,128)(2,1)S(1)}, u32[]{:S(2)}) copy-start(bf16[128,1088]{1,0:T(8,128)(2,1)S(1)} %copy.118) | copy-start | bytes 835588
  11.6 135.4 %copy-start.37 = (f32[128]{0:T(128)}, f32[128]{0:T(128)S(1)}, u32[]{:S(2)}) copy-start(f32[128]{0:T(128)S(1)} %broadcast_multiply_fusion.5) | copy-start | bytes 1540
  11.8 135.2 %copy-start.39 = (f32[128]{0:T(128)}, f32[128]{0:T(128)S(1)}, u32[]{:S(2)}) copy-start(f32[128]{0:T(128)S(1)} %add_rsqrt_fusion.1) | copy-start | bytes 1540
  154.5 2.4 copy-start.35
  155.0 3.3 copy-start.36
  155.9 142.3 %reduce-scatter.4.cloned.1.call-start = ((), (), s32[]{:S(2)}) async-start(), calls=%async_computation.2 | async-start | bytes 2785280
  157.8 10.2 %copy-start.41 = (f32[128]{0:T(128)}, f32[128]{0:T(128)S(1)}, u32[]{:S(2)}) copy-start(f32[128]{0:T(128)S(1)} %get-tuple-element.156) | copy-start | bytes 1540
  158.1 9.9 %copy-start = (bf16[1088,128]{1,0:T(8,128)(2,1)}, bf16[1088,128]{1,0:T(8,128)(2,1)S(1)}, u32[]{:S(2)}) copy-start(bf16[1088,128]{1,0:T(8,128)(2,1)S(1)} %copy.127) | copy-start | bytes 835588
  168.2 2.4 copy-start.43
  170.8 10.4 %copy-start.25 = (bf16[128,1088]{0,1:T(8,128)(2,1)S(1)}, bf16[128,1088]{0,1:T(8,128)(2,1)}, u32[]{:S(2)}) copy-start(bf16[128,1088]{0,1:T(8,128)(2,1)} %slice.115) | copy-start | bytes 835588
  181.1 4.5 copy-start.13
  181.1 4.5 copy-start.7
  188.8 5.5 %copy-start.12 = (bf16[17,64,128]{2,1,0:T(8,128)(2,1)}, bf16[17,64,128]{2,1,0:T(8,128)(2,1)S(1)}, u32[]{:S(2)}) copy-start(bf16[17,64,128]{2,1,0:T(8,128)(2,1)S(1)} %convolution_convert_fusion.2) | copy-start | bytes 835588
  194.7 0.8 copy-start.5
  215.6 8.6 %copy-start.6 = (f32[128,1088]{1,0:T(8,128)S(1)}, f32[128,1088]{1,0:T(8,128)}, u32[]{:S(2)}) copy-start(f32[128,1088]{1,0:T(8,128)} %copy-done.5) | copy-start | bytes 1671172
  224.9 11.2 %copy-start.42 = (f32[128]{0:T(128)S(1)}, f32[128]{0:T(128)}, u32[]{:S(2)}) copy-start(f32[128]{0:T(128)} %copy-done.41) | copy-start | bytes 1540
  233.2 0.8 copy-start.2
  238.4 0.8 copy-start.9
  250.7 2.9 copy-start.8
  250.7 2.9 copy-start.11
  253.7 4.6 copy-start.26
  266.0 0.7 copy-start.38
  266.0 0.7 copy-start.40
  270.4 5.7 %copy-start.1 = (bf16[1088,128]{1,0:T(8,128)(2,1)S(1)}, bf16[1088,128]{1,0:T(8,128)(2,1)}, u32[]{:S(2)}) copy-start(bf16[1088,128]{1,0:T(8,128)(2,1)} %copy-done) | copy-start | bytes 835588
  276.1 12.2 %copy-start.23 = (bf16[1,128,1088]{2,1,0:T(8,128)(2,1)S(1)}, bf16[1,128,1088]{2,1,0:T(8,128)(2,1)}, u32[]{:S(2)}) copy-start(bf16[1,128,1088]{2,1,0:T(8,128)(2,1)} %fusion.97) | copy-start | bytes 835588
  276.1 12.2 %copy-start.24 = (bf16[1,128,1088]{2,1,0:T(8,128)(2,1)S(1)}, bf16[1,128,1088]{2,1,0:T(8,128)(2,1)}, u32[]{:S(2)}) copy-start(bf16[1,128,1088]{2,1,0:T(8,128)(2,1)} %copy.135) | copy-start | bytes 835588
  288.4 11.3 %copy-start.27 = (bf16[128,17,64]{0,2,1:T(8,128)(2,1)S(1)}, bf16[128,17,64]{0,2,1:T(8,128)(2,1)}, u32[]{:S(2)}) copy-start(bf16[128,17,64]{0,2,1:T(8,128)(2,1)} %get-tuple-element.173) | copy-start | bytes 835588
  307.2 1.0 copy-start.4
  475.9 2.1 copy-start.15
  475.9 3.4 copy-start.10
  479.6 2.3 copy-start.14
  481.9 6.4 %copy-start.18 = (f32[544,272]{0,1:T(8,128)}, f32[544,272]{0,1:T(8,128)S(1)}, u32[]{:S(2)}) copy-start(f32[544,272]{0,1:T(8,128)S(1)} %copy.137) | copy-start | bytes 1775620
  481.9 4.9 copy-start.21
  483.0 3.8 copy-start.22
  483.0 3.8 copy-start.32
  483.0 3.8 copy-start.33
  485.2 3.1 copy-start.17
  485.2 3.1 copy-start.28
  485.2 3.1 copy-start.29
  488.3 1.7 copy-start.20
  488.4 1.7 copy-start.30
  488.4 2.1 copy-start.31
  488.4 2.3 copy-start.34
Sparse Core Ops, SparseCore 0:
  156.0 23.3 all-gather.1
  266.1 32.0 reduce-scatter.3
